TPU v7x, 128 devices: a whole 4x4x4 slice. The times are simulated.
128 devices in a mesh: gx: 8 (over y_lo, x), gy: 16 (over z, y_hi, core).
Axes of the slice: x: 4, y: 4 (y_hi: 2, y_lo: 2; y = y_hi * 2 + y_lo), z: 4, core: 2. Of those that a mesh axis runs over, the one named last changes fastest.
Arguments:
- white_noise: float32 [8, 4096, 4096], P('gx', 'gy'), may hold values from -6 to 6
- amplitude: float32 [4096, 4096], P(None, 'gy'), may hold values from 0.24 to 1.26, as said below
- offsets: int32 [2], replicated, may hold values from 0 to 7
Outputs:
- trans_x: float32 [8, 4096, 4096], P('gx', 'gy')
- trans_y: float32 [8, 4096, 4096], P('gx', 'gy')
- upscaled: float32 [512, 512], P('gy', 'gx')
Inputs may be any that keep to these rules, and one draw needn't show every extreme that they name: amplitude[ky, kx] equals amplitude[(4096 - ky) mod 4096, kx] and amplitude[ky, (4096 - kx) mod 4096]. offsets[0] shifts the coarse blocks along y, offsets[1] along x.
All inputs are finite; a program needn't handle non-finite values.
Results may differ from a plain program's by a relative error of at most 0.000096.
Values sent between devices are 32-bit elements; how exact they have to be, the bound alone decides.
A program may use at most 128 MiB of HBM per device.

v0:
```python
import math

import jax
import jax.numpy as jnp
from jax import lax
from jax.sharding import PartitionSpec as P

RADIX = 32


def passed_along(value, axis, steps):
    count = lax.axis_size(axis)
    pairs = [(source, (source + steps) % count) for source in range(count)]
    return lax.ppermute(value, axis, pairs)


def contract(pattern, operand, matrix):
    return jnp.einsum(
        pattern,
        operand,
        matrix,
        precision=lax.Precision.HIGHEST,
        preferred_element_type=jnp.float32,
    )


def angles(count_a, count_b, period):
    left_index = jnp.arange(count_a, dtype=jnp.int32)[:, None]
    right_index = jnp.arange(count_b, dtype=jnp.int32)[None, :]
    reduced = left_index * right_index % period
    return reduced.astype(jnp.float32) * (2.0 * math.pi / period)


def rotate(pattern, real_part, imag_part, cosine, sine_part):
    if imag_part is None:
        return (contract(pattern, real_part, cosine), contract(pattern, real_part, sine_part))
    real_next = contract(pattern, real_part, cosine) - contract(pattern, imag_part, sine_part)
    imag_next = contract(pattern, real_part, sine_part) + contract(pattern, imag_part, cosine)
    return (real_next, imag_next)


def fourier(real_part, imag_part, radix_len, sign_value, middle, real_only):
    axis_pos = real_part.ndim - 2 if middle else real_part.ndim - 1
    length = real_part.shape[axis_pos]
    inner_len = length // radix_len
    lead_shape = real_part.shape[:axis_pos]
    trail_shape = real_part.shape[axis_pos + 1 :]
    split_shape = lead_shape + (radix_len, inner_len) + trail_shape
    whole_shape = lead_shape + (length,) + trail_shape
    real_part = real_part.reshape(split_shape)
    if imag_part is not None:
        imag_part = imag_part.reshape(split_shape)
    first_angle = angles(radix_len, radix_len, radix_len)
    twiddle = angles(radix_len, inner_len, length)
    second = angles(inner_len, inner_len, inner_len)
    if middle:
        form_one = "...abx,ak->...kbx"
        form_two = "...kbx,bm->...mkx"
        twiddle = twiddle[:, :, None]
    else:
        form_one = "...ab,ak->...kb"
        form_two = "...kb,bm->...mk"
    real_part, imag_part = rotate(
        form_one, real_part, imag_part, jnp.cos(first_angle), sign_value * jnp.sin(first_angle)
    )
    cosine = jnp.cos(twiddle)
    sine_part = sign_value * jnp.sin(twiddle)
    real_part, imag_part = (
        real_part * cosine - imag_part * sine_part,
        real_part * sine_part + imag_part * cosine,
    )
    cosine_two = jnp.cos(second)
    sine_two = sign_value * jnp.sin(second)
    if real_only:
        result = contract(form_two, real_part, cosine_two) - contract(form_two, imag_part, sine_two)
        return (result.reshape(whole_shape), None)
    real_part, imag_part = rotate(form_two, real_part, imag_part, cosine_two, sine_two)
    return (real_part.reshape(whole_shape), imag_part.reshape(whole_shape))


def harmonic(first_cell, second_cell):
    return 2.0 * first_cell * second_cell / (first_cell + second_cell)


def shards(white_noise, amplitude, offsets):
    layers, tile_rows, tile_width = white_noise.shape
    full_height = tile_rows * lax.axis_size("gy")
    real_part, imag_part = fourier(white_noise, None, RADIX, -1.0, False, False)
    arrived = lax.all_to_all(
        jnp.stack([real_part, imag_part]), "gy", split_axis=3, concat_axis=2, tiled=True
    )
    real_part, imag_part = fourier(arrived[0], arrived[1], RADIX, -1.0, True, False)
    real_part, imag_part = fourier(
        real_part * amplitude, imag_part * amplitude, RADIX, 1.0, True, False
    )
    arrived = lax.all_to_all(
        jnp.stack([real_part, imag_part]), "gy", split_axis=2, concat_axis=3, tiled=True
    )
    log_field, unused = fourier(arrived[0], arrived[1], RADIX, 1.0, False, True)
    log_field = log_field * (1.0 / (tile_width * full_height))
    permeability = jnp.exp(log_field)
    trans_x = harmonic(permeability, jnp.roll(permeability, -1, axis=2))
    shift_y = offsets[0]
    shift_x = offsets[1]
    column_sums = jnp.stack([jnp.sum(permeability, axis=0), jnp.sum(1.0 / permeability, axis=0)])
    across = (
        jnp.roll(column_sums, -shift_x, axis=2)
        .reshape(2, tile_rows, tile_width // 8, 8)
        .sum(axis=3)
    )
    rolled = jnp.roll(across, -shift_y, axis=1)
    tail_rows = (jnp.arange(tile_rows, dtype=jnp.int32) >= tile_rows - shift_y)[None, :, None]
    kept_rows = jnp.where(tail_rows, 0.0, rolled)
    lead_sums = jnp.sum(jnp.where(tail_rows, rolled, 0.0), axis=1)
    upper_row, upper_lead = passed_along((permeability[:, 0, :], lead_sums), "gy", -1)
    south_cell = jnp.concatenate([permeability[:, 1:, :], upper_row[:, None, :]], axis=1)
    trans_y = harmonic(permeability, south_cell)
    blocks = kept_rows.reshape(2, tile_rows // 8, 8, tile_width // 8).sum(axis=2)
    blocks = blocks.at[:, -1, :].add(upper_lead)
    totals = lax.psum_scatter(blocks, "gx", scatter_dimension=2, tiled=True)
    upscaled = jnp.sqrt(totals[0] / totals[1])
    return (trans_x, trans_y, upscaled)


def solution(mesh):
    return jax.shard_map(
        shards,
        mesh=mesh,
        in_specs=(P("gx", "gy", None), P(None, "gy"), P()),
        out_specs=(P("gx", "gy", None), P("gx", "gy", None), P("gy", "gx")),
        check_vma=False,
    )
```

profile of v0, /device:TPU:0, one launch (start us, length us, event | category | flops | bytes accessed | tf_op | source)
XLA Modules:
  0.0 598.5 jit_solution(5106330993537380140)
XLA Ops:
  7.3 2.9 copy.190
  10.2 4.1 fusion.145
  14.3 4.9 fusion.10
  19.2 6.4 %fusion.51 = f32[128,256,32]{1,0,2:T(8,128)S(1)} fusion(f32[256,32,128]{2,1,0:T(8,128)S(1)} %get-tuple-element.34), kind=kOutput, calls=%fused_computation.78 | convolution fusion | flops 1610858496 | bytes 8388608 | tf_op jit(solution)/shard_map/...kb,bm->...mk/dot_general | solution.py:18
  25.7 6.0 %fusion.49 = f32[128,256,32]{1,0,2:T(8,128)S(1)} fusion(f32[256,32,128]{2,1,0:T(8,128)S(1)} %get-tuple-element.34), kind=kOutput, calls=%fused_computation.76 | convolution fusion | flops 1610842112 | bytes 8388608 | tf_op jit(solution)/shard_map/...kb,bm->...mk/dot_general | solution.py:18
  31.7 6.7 %subtract_bitcast_fusion = f32[1,256,128,32]{1,2,3,0:T(8,128)S(1)} fusion(f32[128,256,32]{1,0,2:T(8,128)S(1)} %fusion.51, f32[256,32,128]{2,1,0:T(8,128)S(1)} %get-tuple-element.33), kind=kOutput, calls=%fused_computation.43 | convolution fusion | flops 1611890688 | bytes 12582912 | tf_op jit(solution)/shard_map/...kb,bm->...mk/dot_general | solution.py:18
  38.4 2.4 copy.144
  40.8 6.5 %add_bitcast_fusion = f32[1,256,128,32]{1,2,3,0:T(8,128)S(1)} fusion(f32[128,256,32]{1,0,2:T(8,128)S(1)} %fusion.49, f32[256,32,128]{2,1,0:T(8,128)S(1)} %get-tuple-element.33), kind=kOutput, calls=%fused_computation.42 | convolution fusion | flops 1611907072 | bytes 12582912 | tf_op jit(solution)/shard_map/...kb,bm->...mk/dot_general | solution.py:18
  47.4 2.4 copy.147
  50.4 22.8 %copy.148 = f32[2,1,256,4096]{2,1,0,3:T(1,128)} copy(f32[2,1,256,4096]{2,3,1,0:T(8,128)S(1)} %pad_maximum_fusion) | data formatting | bytes 16777216 | tf_op jit(solution)/shard_map/stack | solution.py:90
  73.1 8.2 %all-to-all-start = ((f32[2,1,256,4096]{2,1,0,3:T(1,128)}), f32[2,1,256,4096]{2,1,0,3:T(1,128)}, u32[]{:S(2)}, u32[]{:S(2)}) async-start(f32[2,1,256,4096]{2,1,0,3:T(1,128)} %copy.148), calls=%async_computation | async-start | bytes 16777216 | tf_op jit(solution)/shard_map/all_to_all | solution.py:89
  81.7 96.4 %all-to-all-done = f32[2,1,256,4096]{2,1,0,3:T(1,128)} async-done(((f32[2,1,256,4096]{2,1,0,3:T(1,128)}), f32[2,1,256,4096]{2,1,0,3:T(1,128)}, u32[]{:S(2)}, u32[]{:S(2)}) %all-to-all-start) | async-done | bytes 8388640 | tf_op jit(solution)/shard_map/all_to_all | solution.py:89
  178.1 4.0 copy.149
  182.2 4.0 fusion.306
  186.2 5.4 copy.152
  191.5 10.2 %fusion.43 = f32[32,128,256]{2,0,1:T(8,128)} fusion(f32[32,128,256]{2,1,0:T(8,128)} %bitcast.194), kind=kOutput, calls=%fused_computation.70 | convolution fusion | flops 402668544 | bytes 8388608 | tf_op jit(solution)/shard_map/...abx,ak->...kbx/dot_general | solution.py:18
  201.8 7.0 %fusion.41 = f32[32,128,256]{2,0,1:T(8,128)} fusion(f32[32,128,256]{2,1,0:T(8,128)S(1)} %bitcast.195), kind=kOutput, calls=%fused_computation.68 | convolution fusion | flops 402667520 | bytes 8388608 | tf_op jit(solution)/shard_map/...abx,ak->...kbx/dot_general | solution.py:18
  208.7 5.8 copy.150
  214.6 10.0 %fusion.61 = f32[32,128,256]{2,0,1:T(8,128)S(1)} fusion(f32[32,128,256]{2,0,1:T(8,128)} %fusion.43, f32[32,128,256]{2,1,0:T(8,128)} %bitcast.190), kind=kOutput, calls=%fused_computation.84 | convolution fusion | flops 403716096 | bytes 12582912 | tf_op jit(solution)/shard_map/...abx,ak->...kbx/dot_general | solution.py:18
  224.6 7.8 %multiply_subtract_fusion.1 = (f32[32,128,256]{2,0,1:T(8,128)S(1)}, f32[32,128,256]{2,0,1:T(8,128)S(1)}) fusion(f32[32,128,256]{2,0,1:T(8,128)S(1)} %fusion.61, f32[32,128]{0,1:T(8,128)S(1)} %copy.157, f32[32,128]{0,1:T(8,128)S(1)} %copy.154, f32[32,128,256]{2,0,1:T(8,128)S(1)} %copy-done.8, f32[32,128,256]{2,1,0:T(8,128)S(1)} %bitcast.191), kind=kOutput, calls=%fused_computation.41 | convolution fusion | flops 410008576 | bytes 21004288 | tf_op jit(solution)/shard_map/...abx,ak->...kbx/dot_general | solution.py:18
  232.4 6.0 %fusion.33 = f32[128,32,256]{2,0,1:T(8,128)S(1)} fusion(f32[32,128,256]{2,0,1:T(8,128)S(1)} %get-tuple-element.30), kind=kOutput, calls=%fused_computation.60 | convolution fusion | flops 1610842112 | bytes 8388608 | tf_op jit(solution)/shard_map/...kbx,bm->...mkx/dot_general | solution.py:18
  238.4 6.4 %fusion.35 = f32[128,32,256]{2,0,1:T(8,128)S(1)} fusion(f32[32,128,256]{2,0,1:T(8,128)S(1)} %get-tuple-element.30), kind=kOutput, calls=%fused_computation.62 | convolution fusion | flops 1610858496 | bytes 8388608 | tf_op jit(solution)/shard_map/...kbx,bm->...mkx/dot_general | solution.py:18
  244.9 6.4 %fusion.70 = f32[128,32,256]{2,0,1:T(8,128)S(1)} fusion(f32[128,32,256]{2,0,1:T(8,128)S(1)} %fusion.33, f32[32,128,256]{2,0,1:T(8,128)S(1)} %get-tuple-element.29), kind=kOutput, calls=%fused_computation.87 | convolution fusion | flops 1611907072 | bytes 12582912 | tf_op jit(solution)/shard_map/...kbx,bm->...mkx/dot_general | solution.py:18
  251.3 2.4 copy.164
  253.8 6.3 %fusion.67 = f32[128,32,256]{2,0,1:T(8,128)S(1)} fusion(f32[128,32,256]{2,0,1:T(8,128)S(1)} %fusion.35, f32[32,128,256]{2,0,1:T(8,128)S(1)} %get-tuple-element.29), kind=kOutput, calls=%fused_computation.86 | convolution fusion | flops 1611890688 | bytes 12582912 | tf_op jit(solution)/shard_map/...kbx,bm->...mkx/dot_general | solution.py:18
  260.1 4.4 copy.160
  264.5 4.3 bitcast_multiply_fusion.5
  268.8 5.9 fusion.27
  274.7 6.3 %fusion.25 = f32[32,128,256]{2,0,1:T(8,128)S(1)} fusion(f32[32,128,256]{2,1,0:T(8,128)S(1)} %bitcast.193), kind=kOutput, calls=%fused_computation.52 | convolution fusion | flops 402667520 | bytes 8388608 | tf_op jit(solution)/shard_map/...abx,ak->...kbx/dot_general | solution.py:18
  281.0 6.3 %fusion.73 = f32[32,128,256]{2,0,1:T(8,128)S(1)} fusion(f32[32,128,256]{2,0,1:T(8,128)S(1)} %fusion.27, f32[32,128,256]{2,1,0:T(8,128)S(1)} %bitcast.188), kind=kOutput, calls=%fused_computation.88 | convolution fusion | flops 403716096 | bytes 12582912 | tf_op jit(solution)/shard_map/...abx,ak->...kbx/dot_general | solution.py:18
  287.4 7.7 %multiply_subtract_fusion = (f32[32,128,256]{2,0,1:T(8,128)S(1)}, f32[32,128,256]{2,0,1:T(8,128)S(1)}) fusion(f32[32,128,256]{2,0,1:T(8,128)S(1)} %fusion.73, f32[32,128]{0,1:T(8,128)S(1)} %copy.168, f32[32,128]{0,1:T(8,128)S(1)} %copy.154, f32[32,128,256]{2,0,1:T(8,128)S(1)} %fusion.25, f32[32,128,256]{2,1,0:T(8,128)S(1)} %bitcast.189), kind=kOutput, calls=%fused_computation.39 | convolution fusion | flops 410007552 | bytes 21004288 | tf_op jit(solution)/shard_map/...abx,ak->...kbx/dot_general | solution.py:18
  295.1 6.0 %fusion.19 = f32[128,32,256]{2,0,1:T(8,128)S(1)} fusion(f32[32,128,256]{2,0,1:T(8,128)S(1)} %get-tuple-element.28), kind=kOutput, calls=%fused_computation.46 | convolution fusion | flops 1610842112 | bytes 8388608 | tf_op jit(solution)/shard_map/...kbx,bm->...mkx/dot_general | solution.py:18
  301.1 6.2 %fusion.17 = f32[128,32,256]{2,0,1:T(8,128)S(1)} fusion(f32[32,128,256]{2,0,1:T(8,128)S(1)} %get-tuple-element.28), kind=kOutput, calls=%fused_computation.44 | convolution fusion | flops 1610842112 | bytes 8388608 | tf_op jit(solution)/shard_map/...kbx,bm->...mkx/dot_general | solution.py:18
  307.3 6.4 %fusion.79 = f32[128,32,256]{2,0,1:T(8,128)S(1)} fusion(f32[128,32,256]{2,0,1:T(8,128)S(1)} %fusion.19, f32[32,128,256]{2,0,1:T(8,128)S(1)} %get-tuple-element.27), kind=kOutput, calls=%fused_computation.90 | convolution fusion | flops 1611890688 | bytes 12582912 | tf_op jit(solution)/shard_map/...kbx,bm->...mkx/dot_general | solution.py:18
  313.8 2.4 copy.171
  316.2 6.4 %fusion.82 = f32[128,32,256]{2,0,1:T(8,128)S(1)} fusion(f32[128,32,256]{2,0,1:T(8,128)S(1)} %fusion.17, f32[32,128,256]{2,0,1:T(8,128)S(1)} %get-tuple-element.27), kind=kOutput, calls=%fused_computation.91 | convolution fusion | flops 1611890688 | bytes 12582912 | tf_op jit(solution)/shard_map/...kbx,bm->...mkx/dot_general | solution.py:18
  322.6 2.4 copy.174
  325.6 22.8 %copy.175 = f32[2,1,4096,256]{3,1,0,2:T(1,128)} copy(f32[2,1,4096,256]{3,2,1,0:T(8,128)S(1)} %pad_maximum_fusion.1) | data formatting | bytes 16777216 | tf_op jit(solution)/shard_map/stack | solution.py:97
  348.4 4.9 all-to-all-start.1
  354.8 95.3 %all-to-all-done.1 = f32[2,1,4096,256]{3,1,0,2:T(1,128)} async-done(((f32[2,1,4096,256]{3,1,0,2:T(1,128)}), f32[2,1,4096,256]{3,1,0,2:T(1,128)}, u32[]{:S(2)}, u32[]{:S(2)}) %all-to-all-start.1) | async-done | bytes 8388640 | tf_op jit(solution)/shard_map/all_to_all | solution.py:96
  450.0 4.0 copy.176
  454.1 2.7 fusion.305
  456.8 4.4 copy.177
  461.2 4.7 reshape.523
  465.9 8.1 %fusion.138 = f32[32,256,128]{2,0,1:T(8,128)} fusion(f32[256,32,128]{2,1,0:T(8,128)} %reshape.523), kind=kOutput, calls=%fused_computation.147 | convolution fusion | flops 402667520 | bytes 8388608 | tf_op jit(solution)/shard_map/...ab,ak->...kb/dot_general | solution.py:18
  474.0 5.2 fusion.148
  479.2 4.4 copy.178
  483.6 5.1 reshape.524
  488.8 7.9 %convolution_add_fusion = f32[32,256,128]{2,0,1:T(8,128)S(1)} fusion(f32[32,256,128]{2,0,1:T(8,128)} %fusion.138, f32[256,32,128]{2,1,0:T(8,128)} %reshape.524), kind=kOutput, calls=%fused_computation.92 | convolution fusion | flops 403716096 | bytes 12582912 | tf_op jit(solution)/shard_map/...ab,ak->...kb/dot_general | solution.py:18
  496.8 5.1 fusion.6
  501.8 6.4 %fusion.13 = f32[128,256,32]{1,0,2:T(8,128)S(1)} fusion(f32[256,32,128]{2,1,0:T(8,128)S(1)} %get-tuple-element.32), kind=kOutput, calls=%fused_computation.31 | convolution fusion | flops 1610842112 | bytes 8388608 | tf_op jit(solution)/shard_map/...kb,bm->...mk/dot_general | solution.py:18
  508.3 6.6 %exponential_bitcast_fusion = f32[1,256,128,32]{1,2,3,0:T(8,128)S(1)} fusion(f32[128,256,32]{1,0,2:T(8,128)S(1)} %fusion.13, f32[256,32,128]{2,1,0:T(8,128)S(1)} %get-tuple-element.31), kind=kOutput, calls=%fused_computation.37 | convolution fusion | flops 1612939264 | bytes 12582912 | tf_op jit(solution)/shard_map/...kb,bm->...mk/dot_general | solution.py:18
  514.9 2.4 copy.181
  517.3 2.0 copy-done
  522.9 4.6 slice.81
  527.6 3.1 slice.83
  531.4 8.4 %broadcast_divide_fusion = (f32[1,256,4096]{1,2,0:T(8,128)S(1)}, f32[1,256,4096]{1,2,0:T(8,128)}, f32[1,256,4096]{1,2,0:T(8,128)}) fusion(f32[1,256,128,32]{1,3,2,0:T(8,128)} %copy-done, f32[1,256,1]{1,2,0:T(1,128)S(1)} %slice.82, f32[1,256,4095]{1,2,0:T(8,128)} %slice.81, f32[1,1,4096]{1,2,0:T(8,128)S(1)} %copy.182, f32[1,255,4096]{1,2,0:T(8,128)} %slice.83), kind=kLoop, calls=%fused_computation.97 | loop fusion | flops 10485760 | bytes 25165824 | tf_op jit(solution)/shard_map/div | solution.py:105
  539.8 6.2 %fusion.3 = f32[2,256,512]{1,2,0:T(8,128)S(1)} fusion(s32[]{:T(128)S(6)} %select_n.176, f32[1,256,4096]{1,2,0:T(8,128)S(1)} %bitcast.187, f32[1,256,4096]{1,2,0:T(8,128)S(1)} %get-tuple-element.39), kind=kLoop, calls=%fused_computation.7 | loop fusion | flops 8126464 | bytes 9437188 | tf_op jit(solution)/shard_map/reduce_sum | solution.py:109
  546.0 1.3 select_reduce_fusion
  548.9 1.1 collective-permute-done.1
  550.3 1.0 reshape.536
  551.3 5.6 copy.184
  556.9 5.6 copy.185
  562.5 27.2 %reduce-scatter.4.cloned.1.call-done = f32[64,64]{1,0:T(8,128)} async-done(((f32[512,64]{1,0:T(8,128)}), f32[64,64]{1,0:T(8,128)}) %reduce-scatter.4.cloned.1.call-update) | async-done | bytes 16400
  (48 shorter events, 7.5 us)
Async XLA Ops:
  73.1 105.0 %all-to-all-start = ((f32[2,1,256,4096]{2,1,0,3:T(1,128)}), f32[2,1,256,4096]{2,1,0,3:T(1,128)}, u32[]{:S(2)}, u32[]{:S(2)}) async-start(f32[2,1,256,4096]{2,1,0,3:T(1,128)} %copy.148), calls=%async_computation | async-start | bytes 16777216 | tf_op jit(solution)/shard_map/all_to_all | solution.py:89
  191.5 10.2 %copy-start.5 = (f32[1,1,16,256,256]{4,3,2,1,0:T(8,128)S(1)}, f32[1,1,16,256,256]{4,3,2,1,0:T(8,128)}, u32[]{:S(2)}) copy-start(f32[1,1,16,256,256]{4,3,2,1,0:T(8,128)} %copy.152) | copy-start | bytes 12582916
  214.5 10.0 %copy-start.4 = (f32[1,1,16,256,256]{4,3,2,1,0:T(8,128)S(1)}, f32[1,1,16,256,256]{4,3,2,1,0:T(8,128)}, u32[]{:S(2)}) copy-start(f32[1,1,16,256,256]{4,3,2,1,0:T(8,128)} %copy.150) | copy-start | bytes 12582916
  214.5 10.0 %copy-start.8 = (f32[32,128,256]{2,0,1:T(8,128)S(1)}, f32[32,128,256]{2,0,1:T(8,128)}, u32[]{:S(2)}) copy-start(f32[32,128,256]{2,0,1:T(8,128)} %fusion.41) | copy-start | bytes 12582916
  348.4 5.1 copy-start.10
  348.4 101.6 %all-to-all-start.1 = ((f32[2,1,4096,256]{3,1,0,2:T(1,128)}), f32[2,1,4096,256]{3,1,0,2:T(1,128)}, u32[]{:S(2)}, u32[]{:S(2)}) async-start(f32[2,1,4096,256]{3,1,0,2:T(1,128)} %copy.175), calls=%async_computation.1 | async-start | bytes 16777216 | tf_op jit(solution)/shard_map/all_to_all | solution.py:96
  353.3 236.4 %reduce-scatter.4.cloned.1.call-start = ((), (), s32[]{:S(2)}) async-start(), calls=%async_computation.3 | async-start | bytes 294912
  465.9 8.1 %copy-start.6 = (f32[256,32,128]{2,1,0:T(8,128)S(1)}, f32[256,32,128]{2,1,0:T(8,128)}, u32[]{:S(2)}) copy-start(f32[256,32,128]{2,1,0:T(8,128)} %reshape.523) | copy-start | bytes 12582916
  474.0 5.2 copy-start.9
  488.8 7.9 %copy-start.3 = (f32[256,32,128]{2,1,0:T(8,128)S(1)}, f32[256,32,128]{2,1,0:T(8,128)}, u32[]{:S(2)}) copy-start(f32[256,32,128]{2,1,0:T(8,128)} %reshape.524) | copy-start | bytes 12582916
  488.8 7.9 %copy-start.7 = (f32[32,256,128]{2,0,1:T(8,128)S(1)}, f32[32,256,128]{2,0,1:T(8,128)}, u32[]{:S(2)}) copy-start(f32[32,256,128]{2,0,1:T(8,128)} %fusion.148) | copy-start | bytes 12582916
  517.3 2.0 copy-start
  520.2 10.5 %collective-permute-start = (f32[1,4096]{1,0:T(1,128)S(1)}, f32[1,4096]{1,0:T(1,128)S(1)}, u32[]{:S(2)}, u32[]{:S(2)}) collective-permute-start(f32[1,4096]{1,0:T(1,128)S(1)} %bitcast.208), channel_id=1, source_target_pairs={{0,15},{1,0},{2,1},{3,2},{4,3},{5,4},{6,5},{7,6},{8,7},{9,8},{10,9... | collective-permute-start | bytes 49160 | tf_op jit(solution)/shard_map/ppermute | solution.py:14
  522.9 4.7 copy-start.1
  531.4 8.5 %copy-start.2 = (f32[1,256,128,32]{1,3,2,0:T(8,128)S(1)}, f32[1,256,128,32]{1,3,2,0:T(8,128)}, u32[]{:S(2)}) copy-start(f32[1,256,128,32]{1,3,2,0:T(8,128)} %copy-done) | copy-start | bytes 12582916
  547.7 2.3 collective-permute-start.1
Sparse Core Ops, SparseCore 0:
  551.5 38.2 reduce-scatter.3
where the time goes:
time: 608 us; the launch traced here: 598 us
  waiting for transfers between devices  220 us (36%)
  matrix products  186 us (31%)
  local copies, waits for them, and re-layouts  138 us (23%)
  other arithmetic  22.4 us (4%)
  between operations  18.1 us (3%)
  starting transfers between devices  14.3 us (2%)
    dot_general x28, matrix products, contract(): jnp.einsum(pattern, operand, matrix, precision=lax.Precision.HIGHEST, pre...  186 us
    all_to_all x1, waiting for transfers between devices, shards(): lax.all_to_all(jnp.stack([real_part, imag_part]), 'gy', split_axis=3, con...  96.4 us
    all_to_all x1, waiting for transfers between devices, shards(): lax.all_to_all(jnp.stack([real_part, imag_part]), 'gy', split_axis=2, con...  95.3 us
    another operation x2, local copies, waits for them, and re-layouts, shards(): jnp.stack([real_part, imag_part])  45.6 us
    unnamed x2, waiting for transfers between devices  27.2 us
    unnamed x30, local copies, waits for them, and re-layouts  18.4 us
  transfers between devices with their start and end apart: 5, of which 4 were waited for; matrix products, arithmetic and copies ran while one was open for 3% of the time, Pallas kernels for 0%

commit v1 on v0

v1 whole, which is shorter than its diff:
```python
import functools
import math

import jax
import jax.numpy as jnp
import numpy as np
from jax import lax
from jax.experimental import pallas as pl
from jax.experimental.pallas import tpu as pltpu
from jax.sharding import PartitionSpec as P

MESH = pl.DeviceIdType.MESH
F32 = jnp.float32
BF16 = jnp.bfloat16
L = 128
T = 32
N = L * T
SLOTS = 16
PER = 4
CHUNKS = SLOTS // PER
G = 16
GX = 8
ROWS = N // G


def _split_table(m):
    hi = m.astype(jnp.bfloat16)
    lo = (m - hi.astype(np.float64)).astype(jnp.bfloat16)
    return np.stack([np.asarray(hi), np.asarray(lo)])


def tables():
    l = np.arange(L)[:, None]
    k = np.arange(L)[None, :]
    ang = 2.0 * np.pi * ((l * k) % L) / L
    c, s = np.cos(ang), np.sin(ang)
    w_f = np.block([[c, -s], [s, c]])
    w_i = np.block([[c, s], [-s, c]])
    half = L // 2
    s_f = np.zeros((2 * L, 2 * L))
    s_i = np.zeros((2 * L, 2 * L))
    lo = np.arange(half)[None, :]
    hi = np.arange(half, L)[None, :]
    a0 = 2.0 * np.pi * ((l * lo) % L) / L
    a16 = 2.0 * np.pi * ((l * (16 + 32 * hi)) % N) / N
    s_f[:L, :half] = np.cos(a0)
    s_f[:L, L : L + half] = -np.sin(a0)
    s_f[:L, L] = 1.0 - 2.0 * (np.arange(L) % 2)
    s_f[L:, half:L] = np.cos(a16)
    s_f[L:, L + half :] = -np.sin(a16)
    s_i[:half, :L] = 2.0 * np.cos(a0).T
    s_i[L : L + half, :L] = -2.0 * np.sin(a0).T
    s_i[0, :L] = 1.0
    s_i[L, :L] = 1.0 - 2.0 * (np.arange(L) % 2)
    s_i[half:L, L:] = 2.0 * np.cos(a16).T
    s_i[L + half :, L:] = -2.0 * np.sin(a16).T
    mats = np.stack([_split_table(m) for m in (w_f, w_i, s_f.T, s_i)])
    q = np.arange(T)[:, None]
    tw = 2.0 * np.pi * ((q * np.arange(L)[None, :]) % N) / N
    return mats, np.stack([np.cos(tw), -np.sin(tw)]).astype(np.float32)


def times_w(re, im, k, n, sign):
    k %= n
    if k == 0:
        return re, im
    if 4 * k == n:
        return (-im, re) if sign > 0 else (im, -re)
    if 2 * k == n:
        return -re, -im
    r = math.sqrt(0.5)
    if 8 * k == n:
        return ((re - im) * r, (re + im) * r) if sign > 0 else ((re + im) * r, (im - re) * r)
    if 8 * k == 3 * n:
        return ((re + im) * -r, (re - im) * r) if sign > 0 else ((im - re) * r, (re + im) * -r)
    c = math.cos(2.0 * math.pi * k / n)
    s = sign * math.sin(2.0 * math.pi * k / n)
    return re * c - im * s, re * s + im * c


def cfft(vals, sign):
    n = len(vals)
    if n == 1:
        return vals
    even, odd = cfft(vals[0::2], sign), cfft(vals[1::2], sign)
    out = [None] * n
    for k in range(n // 2):
        a, b = even[k]
        c, d = times_w(*odd[k], k, n, sign)
        out[k] = (a + c, b + d)
        out[k + n // 2] = (a - c, b - d)
    return out


def rfft(vals):
    n = len(vals)
    if n == 2:
        return [(vals[0] + vals[1], None), (vals[0] - vals[1], None)]
    even, odd = rfft(vals[0::2]), rfft(vals[1::2])
    out = [None] * (n // 2 + 1)
    for k in range(n // 4 + 1):
        a, b = even[k]
        if k == 0:
            out[0] = (a + odd[0][0], None)
            out[n // 2] = (a - odd[0][0], None)
        elif k == n // 4:
            out[k] = (a, -odd[k][0])
        else:
            c, d = times_w(*odd[k], k, n, -1)
            out[k] = (a + c, b + d)
            out[n // 2 - k] = (a - c, d - b)
    return out


def irfft(bins):
    n = 2 * (len(bins) - 1)
    if n == 2:
        return [bins[0][0] + bins[1][0], bins[0][0] - bins[1][0]]
    even, odd = [None] * (n // 4 + 1), [None] * (n // 4 + 1)
    for k in range(n // 4 + 1):
        a, b = bins[k]
        if k == 0:
            c = bins[n // 2][0]
            even[0], odd[0] = (a + c, None), (a - c, None)
        elif k == n // 4:
            even[k], odd[k] = (2.0 * a, None), (-2.0 * b, None)
        else:
            c, d = bins[n // 2 - k]
            even[k] = (a + c, b - d)
            odd[k] = times_w(a - c, b + d, k, n, 1)
    out = [None] * n
    out[0::2], out[1::2] = irfft(even), irfft(odd)
    return out


def split(v):
    hi = v.astype(BF16)
    return hi, (v - hi.astype(F32)).astype(BF16)


def dot(a, b, nt=False):
    dims = (((1,), (1 if nt else 0,)), ((), ()))
    return lax.dot_general(a, b, dims, preferred_element_type=F32)


def dot3(data, mats, which):
    hi, lo = split(data)
    w_hi, w_lo = mats[which, 0], mats[which, 1]
    return dot(hi, w_hi) + (dot(lo, w_hi) + dot(hi, w_lo))


def field_kernel(
    off, x_hbm, amp_hbm, mats, tw,
    p_hbm, halo_out, up_out,
    x_v, amp_v, a_v, send1, recv1, send2, recv2, z_v, z2_v, amp_t, tmp_t, nyq, nyq_in, pr_v, p_v,
    halo_s, halo_r, bs_main, bs_lead, in_main, in_lead, gsel,
    x_sem, amp_sem, s_sem, r_sem, p_sem, m_sem,
):
    gx, me = lax.axis_index("gx"), lax.axis_index("gy")
    south, north = lax.rem(me + 1, G), lax.rem(me + G - 1, G)

    x_parts = [
        pltpu.make_async_copy(x_hbm.at[pl.ds(64 * i, 64)], x_v.at[pl.ds(64 * i, 64)], x_sem.at[i])
        for i in range(4)
    ]
    for cp in x_parts:
        cp.start()
    amp_parts = [
        pltpu.make_async_copy(amp_hbm.at[:, pl.ds(L * h, L)], amp_v.at[h], amp_sem.at[h]) for h in range(2)
    ]
    for cp in amp_parts:
        cp.start()

    barrier = pltpu.get_barrier_semaphore()
    for o in range(1, G):
        pl.semaphore_signal(barrier, inc=1, device_id={"gy": lax.rem(me + o, G)}, device_id_type=MESH)
    for o in range(1, GX):
        peer = lax.rem(gx + o, GX)
        pl.semaphore_signal(barrier, inc=1, device_id={"gx": peer}, device_id_type=MESH)
        pl.semaphore_signal(barrier, inc=1, device_id={"gx": peer, "gy": south}, device_id_type=MESH)

    def x_tiles(i, carry):
        rows = pl.ds(pl.multiple_of(8 * i, 8), 8)
        bins = rfft([x_v[rows, L * t : L * (t + 1)] for t in range(T)])
        a_v[0, rows, :L] = bins[0][0]
        a_v[0, rows, L:] = bins[T // 2][0]
        for k in range(1, SLOTS):
            a, b = bins[k]
            c, s = tw[0, k : k + 1, :], tw[1, k : k + 1, :]
            a_v[k, rows, :L] = a * c - b * s
            a_v[k, rows, L:] = a * s + b * c
        return carry

    for i in range(4):
        x_parts[i].wait()
        lax.fori_loop(8 * i, 8 * i + 8, x_tiles, 0)

    def peer_copy(src, dst, phase, chunk, o):
        return pltpu.make_async_remote_copy(
            src_ref=src,
            dst_ref=dst,
            send_sem=s_sem.at[phase, chunk, o],
            recv_sem=r_sem.at[phase, chunk, o],
            device_id={"gy": lax.rem(me + o, G)},
            device_id_type=MESH,
        )

    def first_copy(chunk, o):
        d = lax.rem(me + o, G)
        return peer_copy(send1.at[d, pl.ds(PER * chunk, PER)], recv1.at[chunk, me], 0, chunk, o)

    def second_copy(chunk, o):
        d = lax.rem(me + o, G)
        return peer_copy(send2.at[d, pl.ds(PER * chunk, PER)], recv2.at[chunk, me], 1, chunk, o)

    def own_copy(first, chunk):
        src, dst = (send1, recv1) if first else (send2, recv2)
        phase = 0 if first else 1
        return pltpu.make_async_copy(
            src.at[me, pl.ds(PER * chunk, PER)], dst.at[chunk, me], r_sem.at[phase, chunk, 0]
        )

    def x_lanes(slot, carry):
        which = jnp.where(slot == 0, 2, 1)
        hi, lo = split(a_v[slot])
        w_hi, w_lo = mats[which, 0], mats[which, 1]
        o = dot(w_hi, hi, True) + (dot(w_hi, lo, True) + dot(w_lo, hi, True))
        for c in range(2):
            for d in range(G):
                send1[d, slot, c] = o[(c * G + d) * 8 : (c * G + d) * 8 + 8, :]
        return carry

    for chunk in range(CHUNKS):
        lax.fori_loop(PER * chunk, PER * chunk + PER, x_lanes, 0)
        if chunk == 0:
            pl.semaphore_wait(barrier, G - 1 + 2 * (GX - 1))
        for o in range(1, G):
            first_copy(chunk, o).start()
        own_copy(True, chunk).start()

    for cp in amp_parts:
        cp.wait()

    def amp_rows(q, carry):
        for h in range(2):
            block = amp_v[h, pl.ds(q, L, stride=T), :]
            tmp_t[L * h : L * (h + 1), :] = block.T
        first = jnp.where(me < G // 2, tmp_t[pl.ds(0, 8, stride=T), :], tmp_t[pl.ds(16, 8, stride=T), :])
        amp_t[q, 0:8, :] = first * (1.0 / (N * N))
        for k in range(1, SLOTS):
            amp_t[q, 8 * k : 8 * k + 8, :] = tmp_t[pl.ds(k, 8, stride=T), :] * (1.0 / (N * N))
        nyq[q] = tmp_t[0:8, :] * (1.0 / (N * N))
        return carry

    lax.fori_loop(0, T, amp_rows, 0)
    nyq_cp = pltpu.make_async_remote_copy(
        src_ref=nyq, dst_ref=nyq_in, send_sem=m_sem.at[0], recv_sem=m_sem.at[1],
        device_id={"gy": lax.rem(me + G // 2, G)}, device_id_type=MESH,
    )
    nyq_cp.start()
    nyq_cp.wait()

    for chunk in range(CHUNKS):
        for o in range(1, G):
            first_copy(chunk, o).wait_recv()
        own_copy(True, chunk).wait()

        def y_tiles(j, carry, chunk=chunk):
            rows = pl.ds(pl.multiple_of(8 * j, 8), 8)
            vals = [
                tuple(recv1[chunk, t // 2, j, c, :, L * (t % 2) : L * (t % 2 + 1)] for c in range(2))
                for t in range(T)
            ]
            out = cfft(vals, -1)
            for q in range(T):
                a, b = out[q]
                if q > 0:
                    c, s = tw[0, q : q + 1, :], tw[1, q : q + 1, :]
                    a, b = a * c - b * s, a * s + b * c
                z_v[q, rows, :L] = a
                z_v[q, rows, L:] = b
            return carry

        lax.fori_loop(0, PER, y_tiles, 0)

        def y_lanes(b, carry, chunk=chunk):
            qs = pl.ds(8 * b, 8)
            f = dot3(z_v[qs].reshape(8 * 8 * PER, 2 * L), mats, 0)
            amp = amp_t[qs, 8 * PER * chunk : 8 * PER * (chunk + 1), :].reshape(8 * 8 * PER, L)
            filtered = jnp.concatenate([f[:, :L] * amp, f[:, L:] * amp], axis=1)
            z_v[qs] = dot3(filtered, mats, 1).reshape(8, 8 * PER, 2 * L)
            if chunk == 0:

                @pl.when(me == 0)
                def _():
                    other = nyq_in[qs].reshape(64, L)
                    g = f.reshape(8, 8 * PER, 2 * L)[:, :8, :].reshape(64, 2 * L)
                    other = jnp.concatenate([g[:, :L] * other, g[:, L:] * other], axis=1)
                    z2_v[qs] = dot3(other, mats, 1).reshape(8, 8, 2 * L)

            return carry

        lax.fori_loop(0, T // 8, y_lanes, 0)

        def back(get):
            vals = []
            for q in range(T):
                a, b = get(q)
                if q > 0:
                    c, s = tw[0, q : q + 1, :], tw[1, q : q + 1, :]
                    a, b = a * c + b * s, b * c - a * s
                vals.append((a, b))
            return cfft(vals, 1)

        def y_back(j, carry, chunk=chunk):
            rows = pl.ds(pl.multiple_of(8 * j, 8), 8)
            out = back(lambda q: (z_v[q, rows, :L], z_v[q, rows, L:]))
            for t in range(T):
                for c in range(2):
                    send2[t // 2, PER * chunk + j, c, :, L * (t % 2) : L * (t % 2 + 1)] = out[t][c]
            return carry

        lax.fori_loop(0, PER, y_back, 0)
        if chunk == 0:

            @pl.when(me == 0)
            def _():
                out = back(lambda q: (z2_v[q, :, :L], z2_v[q, :, L:]))
                for t in range(T):
                    send2[t // 2, 0, 1, 0:1, L * (t % 2) : L * (t % 2 + 1)] = out[t][1][0:1, :]

        for o in range(1, G):
            second_copy(chunk, o).start()
        own_copy(False, chunk).start()

    for chunk in range(CHUNKS):
        for o in range(1, G):
            second_copy(chunk, o).wait_recv()
        own_copy(False, chunk).wait()

        def x_back(j, carry, chunk=chunk):
            slot = PER * chunk + j
            data = jnp.concatenate(
                [recv2[chunk, d, j, c] for c in range(2) for d in range(G)], axis=0
            )
            which = jnp.where(slot == 0, 3, 1)
            o = dot3(data.T, mats, which)
            a, b = o[:, :L], o[:, L:]
            c, s = tw[0, pl.ds(slot, 1), :], tw[1, pl.ds(slot, 1), :]
            a_v[slot, :, :L] = a * c + b * s
            a_v[slot, :, L:] = b * c - a * s
            return carry

        lax.fori_loop(0, PER, x_back, 0)

    pr_v[:, :, ROWS : ROWS + 8, :] = jnp.zeros((2, T, 8, L), F32)

    def x_last(i, carry):
        rows = pl.ds(pl.multiple_of(8 * i, 8), 8)
        bins = [(a_v[0, rows, :L], None)]
        bins += [(a_v[k, rows, :L], a_v[k, rows, L:]) for k in range(1, SLOTS)]
        bins += [(a_v[0, rows, L:], None)]
        out = irfft(bins)
        for t in range(T):
            p = jnp.exp(out[t])
            p_v[rows, L * t : L * (t + 1)] = p
            pr_v[0, t, rows, :] = p
            pr_v[1, t, rows, :] = 1.0 / p
        return carry

    x_last(0, 0)
    for t in range(T):
        halo_s[t : t + 1, :] = p_v[0:1, L * t : L * (t + 1)]
    halo_cp = pltpu.make_async_remote_copy(
        src_ref=halo_s, dst_ref=halo_r, send_sem=m_sem.at[2], recv_sem=m_sem.at[3],
        device_id={"gy": north}, device_id_type=MESH,
    )
    halo_cp.start()
    p_parts = []
    for i in range(4):
        lax.fori_loop(max(8 * i, 1), 8 * i + 8, x_last, 0)
        cp = pltpu.make_async_copy(p_v.at[pl.ds(64 * i, 64)], p_hbm.at[pl.ds(64 * i, 64)], p_sem.at[i])
        cp.start()
        p_parts.append(cp)

    shift_y, shift_x = off[0], off[1]
    wide = 1024 + L
    gsel[...] = jnp.where(
        (lax.broadcasted_iota(jnp.int32, (wide, L), 0) - shift_x) // 8
        == lax.broadcasted_iota(jnp.int32, (wide, L), 1),
        1.0,
        0.0,
    ).astype(BF16)
    lead_mask = lax.broadcasted_iota(jnp.int32, (8, L), 0) < shift_y
    for v in range(2):

        def y_sums(t, carry, v=v):
            lanes = pl.ds(pl.multiple_of(L * t, L), L)
            total = jnp.zeros((T, L), F32)
            for a in range(8):
                here = pr_v[v, t, pl.ds(a, T, stride=8), :]
                after = pr_v[v, t, pl.ds(a + 8, T, stride=8), :]
                total += jnp.where(a >= shift_y, here, after)
            x_v[40 * v : 40 * v + T, lanes] = total
            x_v[40 * v + T : 40 * v + 40, lanes] = jnp.where(lead_mask, pr_v[v, t, 0:8, :], 0.0)
            return carry

        lax.fori_loop(0, T, y_sums, 0)

    g = gsel[...]
    for b in range(4):
        lanes = [x_v[0:80, 1024 * b : 1024 * (b + 1)]]
        nxt = 1024 * (b + 1) % N
        lanes.append(x_v[0:80, nxt : nxt + L])
        hi, lo = split(jnp.concatenate(lanes, axis=1))
        out = dot(hi, g) + dot(lo, g)
        for v in range(2):
            bs_main[b, v] = out[40 * v : 40 * v + T, :]
            bs_lead[b, v] = out[40 * v + T : 40 * v + 40, :]

    def main_copy(o):
        peer = lax.rem(gx + o, GX)
        return pltpu.make_async_remote_copy(
            src_ref=bs_main.at[peer // 2], dst_ref=in_main.at[gx],
            send_sem=m_sem.at[8 + o], recv_sem=m_sem.at[16 + o],
            device_id={"gx": peer}, device_id_type=MESH,
        )

    def lead_copy(o):
        peer = lax.rem(gx + o, GX)
        return pltpu.make_async_remote_copy(
            src_ref=bs_lead.at[peer // 2], dst_ref=in_lead.at[gx],
            send_sem=m_sem.at[24 + o], recv_sem=m_sem.at[32 + o],
            device_id={"gx": peer, "gy": north}, device_id_type=MESH,
        )

    own_main = pltpu.make_async_copy(bs_main.at[gx // 2], in_main.at[gx], m_sem.at[16])
    own_main.start()
    for o in range(1, GX):
        main_copy(o).start()
    for o in range(GX):
        lead_copy(o).start()

    halo_cp.wait()
    for t in range(T):
        halo_out[0:1, L * t : L * (t + 1)] = halo_r[t : t + 1, :]

    own_main.wait()
    for o in range(1, GX):
        main_copy(o).wait()
    for o in range(GX):
        lead_copy(o).wait()
    sums = []
    last = lax.broadcasted_iota(jnp.int32, (T, L), 0) == T - 1
    for v in range(2):
        main, lead = in_main[0, v], in_lead[0, v]
        for g_ in range(1, GX):
            main += in_main[g_, v]
            lead += in_lead[g_, v]
        lead = jnp.sum(lead, axis=0, keepdims=True)
        sums.append(main + jnp.where(last, jnp.broadcast_to(lead, (T, L)), 0.0))
    up = jnp.sqrt(sums[0] / sums[1])
    up_out[...] = jnp.where(lax.rem(gx, 2) == 0, up[:, : L // 2], up[:, L // 2 :])

    for cp in p_parts:
        cp.wait()
    for chunk in range(CHUNKS):
        for o in range(1, G):
            first_copy(chunk, o).wait_send()
            second_copy(chunk, o).wait_send()


def field(off, x, amp, mats, tw):
    any_spec = pl.BlockSpec(memory_space=pl.ANY)
    vmem = pl.BlockSpec(memory_space=pltpu.VMEM)
    piece = (2, 8, ROWS)
    return pl.pallas_call(
        field_kernel,
        out_shape=(
            jax.ShapeDtypeStruct((ROWS, N), F32),
            jax.ShapeDtypeStruct((1, N), F32),
            jax.ShapeDtypeStruct((T, L // 2), F32),
        ),
        in_specs=[pl.BlockSpec(memory_space=pltpu.SMEM), any_spec, any_spec, vmem, vmem],
        out_specs=(any_spec, vmem, vmem),
        scratch_shapes=[
            pltpu.VMEM((ROWS, N), F32),
            pltpu.VMEM((2, N, L), F32),
            pltpu.VMEM((SLOTS, ROWS, 2 * L), F32),
            pltpu.VMEM((G, SLOTS) + piece, F32),
            pltpu.VMEM((CHUNKS, G, PER) + piece, F32),
            pltpu.VMEM((G, SLOTS) + piece, F32),
            pltpu.VMEM((CHUNKS, G, PER) + piece, F32),
            pltpu.VMEM((T, 8 * PER, 2 * L), F32),
            pltpu.VMEM((T, 8, 2 * L), F32),
            pltpu.VMEM((T, 8 * SLOTS, L), F32),
            pltpu.VMEM((2 * L, L), F32),
            pltpu.VMEM((T, 8, L), F32),
            pltpu.VMEM((T, 8, L), F32),
            pltpu.VMEM((2, T, ROWS + 8, L), F32),
            pltpu.VMEM((ROWS, N), F32),
            pltpu.VMEM((T, L), F32),
            pltpu.VMEM((T, L), F32),
            pltpu.VMEM((4, 2, T, L), F32),
            pltpu.VMEM((4, 2, 8, L), F32),
            pltpu.VMEM((GX, 2, T, L), F32),
            pltpu.VMEM((GX, 2, 8, L), F32),
            pltpu.VMEM((1024 + L, L), BF16),
            pltpu.SemaphoreType.DMA((4,)),
            pltpu.SemaphoreType.DMA((2,)),
            pltpu.SemaphoreType.DMA((2, CHUNKS, G)),
            pltpu.SemaphoreType.DMA((2, CHUNKS, G)),
            pltpu.SemaphoreType.DMA((4,)),
            pltpu.SemaphoreType.DMA((40,)),
        ],
        compiler_params=pltpu.CompilerParams(
            collective_id=0, has_side_effects=True, vmem_limit_bytes=60 << 20
        ),
        name="field",
    )(off, x, amp, mats, tw)


BLOCK = 32


def trans_kernel(p_ref, next_ref, halo_ref, tx_ref, ty_ref):
    p = p_ref[...]
    q = pltpu.roll(p, N - 1, 1)
    tx_ref[...] = 2.0 * p * q / (p + q)
    edge = pl.program_id(0) == pl.num_programs(0) - 1
    row = jnp.where(edge, halo_ref[...], next_ref[0:1, :])
    q = jnp.concatenate([p[1:, :], row], axis=0)
    ty_ref[...] = 2.0 * p * q / (p + q)


def transmissibilities(p, halo):
    steps = ROWS // BLOCK
    block = pl.BlockSpec((BLOCK, N), lambda i: (i, 0))
    after = pl.BlockSpec((8, N), lambda i: (jnp.minimum((i + 1) * (BLOCK // 8), ROWS // 8 - 1), 0))
    return pl.pallas_call(
        trans_kernel,
        grid=(steps,),
        out_shape=(jax.ShapeDtypeStruct((ROWS, N), F32),) * 2,
        in_specs=[block, after, pl.BlockSpec((1, N), lambda i: (0, 0))],
        out_specs=(block, block),
        compiler_params=pltpu.CompilerParams(vmem_limit_bytes=32 << 20),
        name="trans",
    )(p, p, halo)


def shards(white_noise, amplitude, offsets):
    mats, tw = tables()
    p, halo, upscaled = field(offsets, white_noise[0], amplitude, jnp.asarray(mats), jnp.asarray(tw))
    trans_x, trans_y = transmissibilities(p, halo)
    return trans_x[None], trans_y[None], upscaled


def solution(mesh):
    return jax.shard_map(
        shards,
        mesh=mesh,
        in_specs=(P("gx", "gy", None), P(None, "gy"), P()),
        out_specs=(P("gx", "gy", None), P("gx", "gy", None), P("gy", "gx")),
        check_vma=False,
    )
```

time: 608 us -> 139 us (0.23); the launches traced: 598 us -> 137 us
  waiting for transfers between devices: 220 us -> 0 us
  matrix products: 186 us -> 0 us
  local copies, waits for them, and re-layouts: 138 us -> 3.51 us
  Pallas kernels: 0 us -> 133 us
  other arithmetic: 22.4 us -> 0 us
  between operations: 18.1 us -> 0.65 us
  starting transfers between devices: 14.3 us -> 0 us
    all_to_all x2 -> x0, waiting for transfers between devices: 192 us -> none  [the longest x1 96.4 us: shards(): lax.all_to_all(jnp.stack([real_part, imag_part]), 'gy', split_axis=3, con...]
    dot_general x28 -> x0, matrix products: 186 us -> none  [contract(): jnp.einsum(pattern, operand, matrix, precision=lax.Precision.HIGHEST, pre...]
    pallas_call x0 -> x2, Pallas kernels: none -> 133 us  [the longest x1 128 us: field(): pl.pallas_call(field_kernel, out_shape=(jax.ShapeDtypeStruct((ROWS, N), F...]
    another operation x4 -> x0, local copies, waits for them, and re-layouts: 55.4 us -> none  [the longest x2 45.6 us: shards(): jnp.stack([real_part, imag_part])]
    slice x12 -> x0, local copies, waits for them, and re-layouts: 35.9 us -> none  [the longest x3 11.5 us: shards(): log_field, unused = fourier(arrived[0], arrived[1], RADIX, 1.0, False, True)]
    unnamed x2 -> x0, waiting for transfers between devices: 27.2 us -> none
    unnamed x30 -> x7, local copies, waits for them, and re-layouts: 18.4 us -> 3.51 us
    all_to_all x2 -> x0, starting transfers between devices: 13.1 us -> none  [the longest x1 8.18 us: shards(): lax.all_to_all(jnp.stack([real_part, imag_part]), 'gy', split_axis=3, con...]
  transfers between devices with their start and end apart: 5 -> 0, of which waited for: 4 -> 0; matrix products, arithmetic and copies ran while one was open for 3% -> 0% of each run, Pallas kernels for 0% -> 0%
where the time goes in v1:
time: 139 us; the launch traced here: 137 us
  Pallas kernels  133 us (96%)
  local copies, waits for them, and re-layouts  3.51 us (3%)
    pallas_call x1, Pallas kernels, field(): pl.pallas_call(field_kernel, out_shape=(jax.ShapeDtypeStruct((ROWS, N), F...  128 us
    pallas_call x1, Pallas kernels, transmissibilities(): pl.pallas_call(trans_kernel, grid=(steps,), out_shape=(jax.ShapeDtypeStru...  5.19 us
    unnamed x7, local copies, waits for them, and re-layouts  3.51 us

profile of v1, /device:TPU:0, one launch (start us, length us, event | category | flops | bytes accessed | tf_op | source)
XLA Modules:
  0.0 137.5 jit_solution(2977246951214486145)
XLA Ops:
  0.6 128.1 %field.1 = (f32[256,4096]{1,0:T(8,128)}, f32[1,4096]{1,0:T(1,128)}, f32[32,64]{1,0:T(8,128)}) custom-call(s32[2]{0:T(128)} %off.1, f32[256,4096]{1,0:T(8,128)} %bitcast.3, f32[4096,256]{1,0:T(8,128)} %amp_hbm.1, bf16[4,2,256,256]{3,2,1,0:T(8,128)(2,1)} %constant.4.clone.mats, f32[2,32,128]{2,1,0:T(8,128)} %constant.5.clone.tw), custom_call_target="tpu_custom_call" | custom-call | tf_op jit(solution)/shard_map/field/pallas_call | solution.py:477
  128.8 0.0 copy-start
  128.8 2.2 %copy-done = f32[256,4096]{1,0:T(8,128)S(1)} copy-done((f32[256,4096]{1,0:T(8,128)S(1)}, f32[256,4096]{1,0:T(8,128)}, u32[]{:S(2)}) %copy-start) | copy-done | bytes 4194328
  130.9 0.0 copy-start.1
  130.9 0.7 copy-done.1
  131.7 0.0 copy-start.2
  131.7 5.2 %trans.1 = (f32[256,4096]{1,0:T(8,128)}, f32[256,4096]{1,0:T(8,128)}) custom-call(f32[256,4096]{1,0:T(8,128)S(1)} %copy-done, f32[256,4096]{1,0:T(8,128)S(1)} %copy-done, f32[1,4096]{1,0:T(1,128)S(1)} %copy-done.1), custom_call_target="tpu_custom_call" | custom-call | tf_op jit(solution)/shard_map/trans/pallas_call | solution.py:540
  136.9 0.0 copy-done.2
  136.9 0.6 copy.9
Async XLA Ops:
  128.8 2.2 %copy-start = (f32[256,4096]{1,0:T(8,128)S(1)}, f32[256,4096]{1,0:T(8,128)}, u32[]{:S(2)}) copy-start(f32[256,4096]{1,0:T(8,128)} %get-tuple-element.8.p_ref.next_ref) | copy-start | bytes 12582916
  130.9 0.7 copy-start.1
  131.7 5.2 %copy-start.2 = (f32[32,64]{1,0:T(8,128)S(1)}, f32[32,64]{1,0:T(8,128)}, u32[]{:S(2)}) copy-start(f32[32,64]{1,0:T(8,128)} %get-tuple-element.18) | copy-start | bytes 24580

commit v2 on v1

v2 whole, which is shorter than its diff:
```python
import functools
import math

import jax
import jax.numpy as jnp
import numpy as np
from jax import lax
from jax.experimental import pallas as pl
from jax.experimental.pallas import tpu as pltpu
from jax.sharding import PartitionSpec as P

MESH = pl.DeviceIdType.MESH
F32 = jnp.float32
BF16 = jnp.bfloat16
L = 128
T = 32
N = L * T
SLOTS = 16
PER = 4
CHUNKS = SLOTS // PER
G = 16
GX = 8
ROWS = N // G
ORDER = [2, 4, 12, 14, 8, 6, 10, 3, 13, 5, 11, 9, 7, 15, 1]


def _split_table(m):
    hi = m.astype(jnp.bfloat16)
    lo = (m - hi.astype(np.float64)).astype(jnp.bfloat16)
    return np.stack([np.asarray(hi), np.asarray(lo)])


def tables():
    l = np.arange(L)[:, None]
    k = np.arange(L)[None, :]
    ang = 2.0 * np.pi * ((l * k) % L) / L
    c, s = np.cos(ang), np.sin(ang)
    w_f = np.block([[c, -s], [s, c]])
    w_i = np.block([[c, s], [-s, c]])
    half = L // 2
    s_f = np.zeros((2 * L, 2 * L))
    s_i = np.zeros((2 * L, 2 * L))
    lo = np.arange(half)[None, :]
    hi = np.arange(half, L)[None, :]
    a0 = 2.0 * np.pi * ((l * lo) % L) / L
    a16 = 2.0 * np.pi * ((l * (16 + 32 * hi)) % N) / N
    s_f[:L, :half] = np.cos(a0)
    s_f[:L, L : L + half] = -np.sin(a0)
    s_f[:L, L] = 1.0 - 2.0 * (np.arange(L) % 2)
    s_f[L:, half:L] = np.cos(a16)
    s_f[L:, L + half :] = -np.sin(a16)
    s_i[:half, :L] = 2.0 * np.cos(a0).T
    s_i[L : L + half, :L] = -2.0 * np.sin(a0).T
    s_i[0, :L] = 1.0
    s_i[L, :L] = 1.0 - 2.0 * (np.arange(L) % 2)
    s_i[half:L, L:] = 2.0 * np.cos(a16).T
    s_i[L + half :, L:] = -2.0 * np.sin(a16).T
    mats = np.stack([_split_table(m) for m in (w_f, w_i, s_f.T, s_i)])
    q = np.arange(T)[:, None]
    tw = 2.0 * np.pi * ((q * np.arange(L)[None, :]) % N) / N
    return mats, np.stack([np.cos(tw), -np.sin(tw)]).astype(np.float32)


def slot_of(chunk, j):
    return PER * ((chunk + 1) % CHUNKS) + j


def times_w(re, im, k, n, sign):
    k %= n
    if k == 0:
        return re, im
    if 4 * k == n:
        return (-im, re) if sign > 0 else (im, -re)
    if 2 * k == n:
        return -re, -im
    r = math.sqrt(0.5)
    if 8 * k == n:
        return ((re - im) * r, (re + im) * r) if sign > 0 else ((re + im) * r, (im - re) * r)
    if 8 * k == 3 * n:
        return ((re + im) * -r, (re - im) * r) if sign > 0 else ((im - re) * r, (re + im) * -r)
    c = math.cos(2.0 * math.pi * k / n)
    s = sign * math.sin(2.0 * math.pi * k / n)
    return re * c - im * s, re * s + im * c


def cfft(vals, sign):
    n = len(vals)
    if n == 1:
        return vals
    even, odd = cfft(vals[0::2], sign), cfft(vals[1::2], sign)
    out = [None] * n
    for k in range(n // 2):
        a, b = even[k]
        c, d = times_w(*odd[k], k, n, sign)
        out[k] = (a + c, b + d)
        out[k + n // 2] = (a - c, b - d)
    return out


def rfft(vals):
    n = len(vals)
    if n == 2:
        return [(vals[0] + vals[1], None), (vals[0] - vals[1], None)]
    even, odd = rfft(vals[0::2]), rfft(vals[1::2])
    out = [None] * (n // 2 + 1)
    for k in range(n // 4 + 1):
        a, b = even[k]
        if k == 0:
            out[0] = (a + odd[0][0], None)
            out[n // 2] = (a - odd[0][0], None)
        elif k == n // 4:
            out[k] = (a, -odd[k][0])
        else:
            c, d = times_w(*odd[k], k, n, -1)
            out[k] = (a + c, b + d)
            out[n // 2 - k] = (a - c, d - b)
    return out


def irfft(bins):
    n = 2 * (len(bins) - 1)
    if n == 2:
        return [bins[0][0] + bins[1][0], bins[0][0] - bins[1][0]]
    even, odd = [None] * (n // 4 + 1), [None] * (n // 4 + 1)
    for k in range(n // 4 + 1):
        a, b = bins[k]
        if k == 0:
            c = bins[n // 2][0]
            even[0], odd[0] = (a + c, None), (a - c, None)
        elif k == n // 4:
            even[k], odd[k] = (2.0 * a, None), (-2.0 * b, None)
        else:
            c, d = bins[n // 2 - k]
            even[k] = (a + c, b - d)
            odd[k] = times_w(a - c, b + d, k, n, 1)
    out = [None] * n
    out[0::2], out[1::2] = irfft(even), irfft(odd)
    return out


def split(v):
    hi = v.astype(BF16)
    return hi, (v - hi.astype(F32)).astype(BF16)


def dot(a, b, nt=False):
    dims = (((1,), (1 if nt else 0,)), ((), ()))
    return lax.dot_general(a, b, dims, preferred_element_type=F32)


def dot3(data, mats, which):
    hi, lo = split(data)
    w_hi, w_lo = mats[which, 0], mats[which, 1]
    return dot(hi, w_hi) + (dot(lo, w_hi) + dot(hi, w_lo))


def field_kernel(
    off_hbm, x_hbm, amp_hbm, mats_hbm, tw_hbm,
    tx_out, ty_out, ratio_out,
    off, tw, mats, p_v, a_v, send1, recv1, send2, recv2, z_v, z2_v, amp_t, tmp_t, nyq, nyq_in, pr_v,
    up_s, low_s, sum_s, halo_s, halo_r, bs_main, in_main, gsel,
    x_sem, amp_sem, s1_sem, r1_sem, s2_sem, r2_sem, m_sem,
):
    gx, me = lax.axis_index("gx"), lax.axis_index("gy")
    north = lax.rem(me + G - 1, G)

    barrier = pltpu.get_barrier_semaphore()
    for o in ORDER:
        pl.semaphore_signal(barrier, inc=1, device_id={"gy": lax.rem(me + o, G)}, device_id_type=MESH)
    for o in range(1, GX):
        pl.semaphore_signal(barrier, inc=1, device_id={"gx": lax.rem(gx + o, GX)}, device_id_type=MESH)

    x_parts = [
        pltpu.make_async_copy(x_hbm.at[pl.ds(32 * i, 32)], p_v.at[pl.ds(32 * i, 32)], x_sem.at[i])
        for i in range(8)
    ]
    mats_cp = pltpu.make_async_copy(mats_hbm, mats, amp_sem.at[2])
    tw_cp = pltpu.make_async_copy(tw_hbm, tw, amp_sem.at[3])
    off_cp = pltpu.make_async_copy(off_hbm, off, amp_sem.at[4])
    x_parts[0].start()
    tw_cp.start()
    x_parts[1].start()
    mats_cp.start()
    off_cp.start()
    for cp in x_parts[2:]:
        cp.start()
    amp_parts = [
        pltpu.make_async_copy(amp_hbm.at[:, pl.ds(L * h, L)], pr_v.at[0, pl.ds(N * h, N)], amp_sem.at[h]) for h in range(2)
    ]
    for cp in amp_parts:
        cp.start()

    def x_tiles(i, carry):
        rows = pl.ds(pl.multiple_of(8 * i, 8), 8)
        bins = rfft([p_v[rows, L * t : L * (t + 1)] for t in range(T)])
        a_v[0, rows, :L] = bins[0][0]
        a_v[0, rows, L:] = bins[T // 2][0]
        for k in range(1, SLOTS):
            a, b = bins[k]
            c, s = tw[0, k : k + 1, :], tw[1, k : k + 1, :]
            a_v[k, rows, :L] = a * c - b * s
            a_v[k, rows, L:] = a * s + b * c
        return carry

    def first_copy(chunk, o):
        d = lax.rem(me + o, G)
        return pltpu.make_async_remote_copy(
            src_ref=send1.at[d, chunk], dst_ref=recv1.at[chunk, me],
            send_sem=s1_sem.at[chunk, o], recv_sem=r1_sem.at[chunk, o],
            device_id={"gy": d}, device_id_type=MESH,
        )

    def first_own(chunk):
        return pltpu.make_async_copy(send1.at[me, chunk], recv1.at[chunk, me], r1_sem.at[chunk, 0])

    def send_first(chunk):
        for o in ORDER:
            first_copy(chunk, o).start()
        first_own(chunk).start()

    def second_copy(half, chunk, o):
        d = lax.rem(me + o, G)
        return pltpu.make_async_remote_copy(
            src_ref=send2.at[d, half, chunk], dst_ref=recv2.at[half, chunk, me],
            send_sem=s2_sem.at[half, chunk, o], recv_sem=r2_sem.at[half, chunk, o],
            device_id={"gy": d}, device_id_type=MESH,
        )

    def second_own(half, chunk):
        return pltpu.make_async_copy(
            send2.at[me, half, chunk], recv2.at[half, chunk, me], r2_sem.at[half, chunk, 0]
        )

    def send_second(half, chunk):
        for o in ORDER:
            second_copy(half, chunk, o).start()
        second_own(half, chunk).start()

    def x_lanes(j, carry, chunk):
        slot = slot_of(chunk, j)
        which = jnp.where(slot == 0, 2, 1)
        hi, lo = split(a_v[slot])
        w_hi, w_lo = mats[which, 0], mats[which, 1]
        o = dot(w_hi, hi, True) + (dot(w_hi, lo, True) + dot(w_lo, hi, True))
        for h in range(2):
            for c in range(2):
                for d in range(G):
                    r = (c * G + d) * 8
                    send1[d, chunk, h, j, c] = o[r : r + 8, L * h : L * (h + 1)]
        return carry

    for i in range(8):
        x_parts[i].wait()
        if i == 0:
            tw_cp.wait()
        lax.fori_loop(4 * i, 4 * i + 4, x_tiles, 0)
    mats_cp.wait()
    off_cp.wait()
    for chunk in range(CHUNKS):
        lax.fori_loop(0, PER, functools.partial(x_lanes, chunk=chunk), 0)
        if chunk == 0:
            pl.semaphore_wait(barrier, G - 1 + GX - 1)
        send_first(chunk)

    for cp in amp_parts:
        cp.wait()

    def amp_rows(q, carry):
        for h in range(2):
            block = pr_v[0, pl.ds(N * h + q, L, stride=T), :]
            tmp_t[L * h : L * (h + 1), :] = block.T
        first = jnp.where(me < G // 2, tmp_t[pl.ds(0, 8, stride=T), :], tmp_t[pl.ds(16, 8, stride=T), :])
        amp_t[q, 0:8, :] = first * (1.0 / (N * N))
        for k in range(1, SLOTS):
            amp_t[q, 8 * k : 8 * k + 8, :] = tmp_t[pl.ds(k, 8, stride=T), :] * (1.0 / (N * N))
        nyq[pl.ds(q, 1), :] = tmp_t[0:1, :] * (1.0 / (N * N))
        return carry

    lax.fori_loop(0, T, amp_rows, 0)
    nyq_cp = pltpu.make_async_remote_copy(
        src_ref=nyq, dst_ref=nyq_in, send_sem=m_sem.at[0], recv_sem=m_sem.at[1],
        device_id={"gy": 0}, device_id_type=MESH,
    )

    @pl.when(me == G // 2)
    def _():
        nyq_cp.start()
        nyq_cp.wait_send()


    shift_y, shift_x = off[0], off[1]
    wide = 1024 + L
    gsel[...] = jnp.where(
        (lax.broadcasted_iota(jnp.int32, (wide, L), 0) - shift_x) // 8
        == lax.broadcasted_iota(jnp.int32, (wide, L), 1),
        1.0,
        0.0,
    ).astype(BF16)

    for chunk in range(CHUNKS):
        for o in ORDER:
            first_copy(chunk, o).wait_recv()
        first_own(chunk).wait()

        def y_tiles(j, carry, chunk=chunk):
            rows = pl.ds(pl.multiple_of(8 * j, 8), 8)
            vals = [tuple(recv1[chunk, t // 2, t % 2, j, c] for c in range(2)) for t in range(T)]
            out = cfft(vals, -1)
            for q in range(T):
                a, b = out[q]
                if q > 0:
                    c, s = tw[0, q : q + 1, :], tw[1, q : q + 1, :]
                    a, b = a * c - b * s, a * s + b * c
                z_v[q, rows, :L] = a
                z_v[q, rows, L:] = b
            return carry

        lax.fori_loop(0, PER, y_tiles, 0)
        if chunk == CHUNKS - 1:

            @pl.when(me == 0)
            def _():
                nyq_cp.wait_recv()

        def y_lanes(b, carry, chunk=chunk):
            qs = pl.ds(8 * b, 8)
            f = dot3(z_v[qs].reshape(8 * 8 * PER, 2 * L), mats, 0)
            first = 8 * slot_of(chunk, 0)
            amp = amp_t[qs, first : first + 8 * PER, :].reshape(8 * 8 * PER, L)
            filtered = jnp.concatenate([f[:, :L] * amp, f[:, L:] * amp], axis=1)
            z_v[qs] = dot3(filtered, mats, 1).reshape(8, 8 * PER, 2 * L)
            if chunk == CHUNKS - 1:

                @pl.when(me == 0)
                def _():
                    other = nyq_in[qs]
                    other = jnp.broadcast_to(other[:, None, :], (8, 8, L)).reshape(64, L)
                    g = f.reshape(8, 8 * PER, 2 * L)[:, :8, :].reshape(64, 2 * L)
                    other = jnp.concatenate([g[:, :L] * other, g[:, L:] * other], axis=1)
                    z2_v[qs] = dot3(other, mats, 1).reshape(8, 8, 2 * L)

            return carry

        lax.fori_loop(0, T // 8, y_lanes, 0)

        def back(get):
            vals = []
            for q in range(T):
                a, b = get(q)
                if q > 0:
                    c, s = tw[0, q : q + 1, :], tw[1, q : q + 1, :]
                    a, b = a * c + b * s, b * c - a * s
                vals.append((a, b))
            return cfft(vals, 1)

        def y_back(j, carry, chunk=chunk):
            rows = pl.ds(pl.multiple_of(8 * j, 8), 8)
            out = back(lambda q: (z_v[q, rows, :L], z_v[q, rows, L:]))
            for t in range(T):
                for c in range(2):
                    send2[t // 2, t % 2, chunk, j, c] = out[t][c]
            return carry

        lax.fori_loop(0, PER, y_back, 0)
        if chunk == CHUNKS - 1:

            @pl.when(me == 0)
            def _():
                out = back(lambda q: (z2_v[q, :, :L], z2_v[q, :, L:]))
                for t in range(T):
                    send2[t // 2, t % 2, CHUNKS - 1, 0, 1, 0:1, :] = out[t][1][0:1, :]

        send_second(0, chunk)
    for chunk in range(CHUNKS):
        send_second(1, chunk)

    def x_back(j, carry, half, chunk):
        slot = slot_of(chunk, j)
        data = jnp.concatenate(
            [recv2[half, chunk, d, j, c] for c in range(2) for d in range(G)], axis=0
        )
        which = jnp.where(slot == 0, 3, 1)
        o = dot3(data.T, mats, which)
        a, b = o[:, :L], o[:, L:]
        c, s = tw[0, pl.ds(slot, 1), :], tw[1, pl.ds(slot, 1), :]
        a_v[slot, L * half : L * (half + 1), :L] = a * c + b * s
        a_v[slot, L * half : L * (half + 1), L:] = b * c - a * s
        return carry

    def x_last(i, carry):
        rows = pl.ds(pl.multiple_of(8 * i, 8), 8)
        bins = [(a_v[0, rows, :L], None)]
        bins += [(a_v[k, rows, :L], a_v[k, rows, L:]) for k in range(1, SLOTS)]
        bins += [(a_v[0, rows, L:], None)]
        out = irfft(bins)
        for t in range(T):
            p = jnp.exp(out[t])
            p_v[rows, L * t : L * (t + 1)] = p
            here = pl.ds(pl.multiple_of(ROWS * t + 8 * i, 8), 8)
            pr_v[0, here, :] = p
            pr_v[1, here, :] = 1.0 / p
        return carry

    def y_sums(t, carry, half):
        for v in range(2):
            up, low = jnp.zeros((16, L), F32), jnp.zeros((16, L), F32)
            for a in range(8):
                u = pr_v[v, pl.ds(ROWS * t + L * half + a, 16, stride=8), :]
                up += jnp.where(a >= shift_y, u, 0.0)
                low += jnp.where(a < shift_y, u, 0.0)
            up_s[v, t, 16 * half : 16 * half + 16, :] = up
            low_s[v, t, 16 * half : 16 * half + 16, :] = low
        return carry

    lane_end = lax.broadcasted_iota(jnp.int32, (8, L), 1) == L - 1

    def trans(i, carry):
        rows = pl.ds(pl.multiple_of(8 * i, 8), 8)
        after = pl.ds(pl.multiple_of(8 * i + 8, 8), 8)
        p = [p_v[rows, L * t : L * (t + 1)] for t in range(T)]
        rolled = [pltpu.roll(v, L - 1, 1) for v in p]
        for t in range(T):
            lanes = slice(L * t, L * (t + 1))
            q = jnp.where(lane_end, rolled[(t + 1) % T], rolled[t])
            tx_out[rows, lanes] = 2.0 * p[t] * q / (p[t] + q)
            q = jnp.concatenate([p[t], p_v[after, lanes]], axis=0)[1:9]
            ty_out[rows, lanes] = 2.0 * p[t] * q / (p[t] + q)
        return carry

    halo_cp = pltpu.make_async_remote_copy(
        src_ref=halo_s, dst_ref=halo_r, send_sem=m_sem.at[2], recv_sem=m_sem.at[3],
        device_id={"gy": north}, device_id_type=MESH,
    )
    g = gsel[...]

    def along_x(rows):
        outs = []
        for b in range(4):
            nxt = 1024 * (b + 1) % N
            lanes = [sum_s[rows, 1024 * b : 1024 * (b + 1)], sum_s[rows, nxt : nxt + L]]
            hi, lo = split(jnp.concatenate(lanes, axis=1))
            outs.append(dot(hi, g) + dot(lo, g))
        return outs

    last_row = lax.broadcasted_iota(jnp.int32, (T, L), 0) == T - 1
    for half in range(2):
        for chunk in range(CHUNKS):
            for o in ORDER:
                second_copy(half, chunk, o).wait_recv()
            second_own(half, chunk).wait()
            lax.fori_loop(0, PER, functools.partial(x_back, half=half, chunk=chunk), 0)
        lax.fori_loop(16 * half, 16 * half + 16, x_last, 0)
        lax.fori_loop(0, T, functools.partial(y_sums, half=half), 0)
        if half == 0:
            for t in range(T):
                halo_s[t : t + 1, :] = p_v[0:1, L * t : L * (t + 1)]
                for v in range(2):
                    sum_s[v : v + 1, L * t : L * (t + 1)] = low_s[v, t, 0:1, :]
            sum_s[2:8, :] = jnp.zeros((6, N), F32)
            for b, out in enumerate(along_x(slice(0, 8))):
                halo_s[T + 2 * b : T + 2 * b + 2, :] = out[0:2]
            halo_cp.start()
            lax.fori_loop(0, 15, trans, 0)

    for t in range(T):
        for v in range(2):
            moved = jnp.where(last_row, 0.0, pltpu.roll(low_s[v, t], T - 1, 0))
            sum_s[T * v : T * v + T, L * t : L * (t + 1)] = up_s[v, t] + moved
    halo_cp.wait()
    for b, out in enumerate(along_x(slice(0, 2 * T))):
        for v in range(2):
            lead = jnp.broadcast_to(halo_r[T + 2 * b + v : T + 2 * b + v + 1, :], (T, L))
            bs_main[b, v] = out[T * v : T * v + T, :] + jnp.where(last_row, lead, 0.0)

    def main_copy(o):
        peer = lax.rem(gx + o, GX)
        return pltpu.make_async_remote_copy(
            src_ref=bs_main.at[peer // 2], dst_ref=in_main.at[gx],
            send_sem=m_sem.at[8 + o], recv_sem=m_sem.at[16 + o],
            device_id={"gx": peer}, device_id_type=MESH,
        )

    own_main = pltpu.make_async_copy(bs_main.at[gx // 2], in_main.at[gx], m_sem.at[16])
    own_main.start()
    for o in range(1, GX):
        main_copy(o).start()
    for t in range(T):
        p_v[ROWS : ROWS + 1, L * t : L * (t + 1)] = halo_r[t : t + 1, :]

    lax.fori_loop(15, 32, trans, 0)
    for chunk in range(CHUNKS):
        for o in ORDER:
            first_copy(chunk, o).wait_send()
    for half in range(2):
        for chunk in range(CHUNKS):
            for o in ORDER:
                second_copy(half, chunk, o).wait_send()

    own_main.wait()
    for o in range(1, GX):
        main_copy(o).wait()
    sums = []
    for v in range(2):
        main = in_main[0, v]
        for g_ in range(1, GX):
            main += in_main[g_, v]
        sums.append(main)
    ratio = sums[0] / sums[1]
    ratio_out[...] = jnp.where(lax.rem(gx, 2) == 0, ratio[:, : L // 2], ratio[:, L // 2 :])


def field(off, x, amp, mats, tw):
    hbm = pl.BlockSpec(memory_space=pltpu.HBM)
    vmem = pl.BlockSpec(memory_space=pltpu.VMEM)
    piece = (PER, 2, 8, L)
    return pl.pallas_call(
        field_kernel,
        out_shape=(
            jax.ShapeDtypeStruct((ROWS, N), F32),
            jax.ShapeDtypeStruct((ROWS, N), F32),
            jax.ShapeDtypeStruct((T, L // 2), F32),
        ),
        in_specs=[hbm] * 5,
        out_specs=(vmem, vmem, vmem),
        scratch_shapes=[
            pltpu.SMEM((2,), jnp.int32),
            pltpu.VMEM(tw.shape, F32),
            pltpu.VMEM(mats.shape, BF16),
            pltpu.VMEM((ROWS + 8, N), F32),
            pltpu.VMEM((SLOTS, ROWS, 2 * L), F32),
            pltpu.VMEM((G, CHUNKS, 2) + piece, F32),
            pltpu.VMEM((CHUNKS, G, 2) + piece, F32),
            pltpu.VMEM((G, 2, CHUNKS) + piece, F32),
            pltpu.VMEM((2, CHUNKS, G) + piece, F32),
            pltpu.VMEM((T, 8 * PER, 2 * L), F32),
            pltpu.VMEM((T, 8, 2 * L), F32),
            pltpu.VMEM((T, 8 * SLOTS, L), F32),
            pltpu.VMEM((2 * L, L), F32),
            pltpu.VMEM((T, L), F32),
            pltpu.VMEM((T, L), F32),
            pltpu.VMEM((2, T * ROWS, L), F32),
            pltpu.VMEM((2, T, T, L), F32),
            pltpu.VMEM((2, T, T, L), F32),
            pltpu.VMEM((2 * T, N), F32),
            pltpu.VMEM((T + 8, L), F32),
            pltpu.VMEM((T + 8, L), F32),
            pltpu.VMEM((4, 2, T, L), F32),
            pltpu.VMEM((GX, 2, T, L), F32),
            pltpu.VMEM((1024 + L, L), BF16),
            pltpu.SemaphoreType.DMA((8,)),
            pltpu.SemaphoreType.DMA((5,)),
            pltpu.SemaphoreType.DMA((CHUNKS, G)),
            pltpu.SemaphoreType.DMA((CHUNKS, G)),
            pltpu.SemaphoreType.DMA((2, CHUNKS, G)),
            pltpu.SemaphoreType.DMA((2, CHUNKS, G)),
            pltpu.SemaphoreType.DMA((24,)),
        ],
        compiler_params=pltpu.CompilerParams(
            collective_id=0, has_side_effects=True, vmem_limit_bytes=44 << 20
        ),
        name="field",
    )(*(pltpu.with_memory_space_constraint(v, pltpu.HBM) for v in (off, x, amp, mats, tw)))


def write_kernel(tx, ty, ratio, tx_out, ty_out, up_out, sem):
    copies = []
    for n, (src, dst) in enumerate(((tx, tx_out), (ty, ty_out))):
        for i in range(4):
            rows = pl.ds(ROWS // 4 * i, ROWS // 4)
            copies.append(pltpu.make_async_copy(src.at[rows], dst.at[rows], sem.at[4 * n + i]))
    for cp in copies:
        cp.start()
    up_out[...] = jnp.sqrt(ratio[...])
    for cp in copies:
        cp.wait()


def written(tx, ty, ratio):
    hbm = pl.BlockSpec(memory_space=pltpu.HBM)
    vmem = pl.BlockSpec(memory_space=pltpu.VMEM)
    return pl.pallas_call(
        write_kernel,
        out_shape=(
            jax.ShapeDtypeStruct((ROWS, N), F32),
            jax.ShapeDtypeStruct((ROWS, N), F32),
            jax.ShapeDtypeStruct((T, L // 2), F32),
        ),
        in_specs=[pl.BlockSpec(memory_space=pl.ANY)] * 2 + [vmem],
        out_specs=(hbm, hbm, vmem),
        scratch_shapes=[pltpu.SemaphoreType.DMA((8,))],
        compiler_params=pltpu.CompilerParams(vmem_limit_bytes=1 << 20),
        name="write",
    )(tx, ty, ratio)


def shards(white_noise, amplitude, offsets):
    mats, tw = tables()
    tx, ty, ratio = field(offsets, white_noise[0], amplitude, jnp.asarray(mats), jnp.asarray(tw))
    trans_x, trans_y, upscaled = written(tx, ty, ratio)
    return trans_x[None], trans_y[None], upscaled


def solution(mesh):
    return jax.shard_map(
        shards,
        mesh=mesh,
        in_specs=(P("gx", "gy", None), P(None, "gy"), P()),
        out_specs=(P("gx", "gy", None), P("gx", "gy", None), P("gy", "gx")),
        check_vma=False,
    )
```

time: 139 us -> 121 us (0.87)
  Pallas kernels: 133 us -> 120 us
  local copies, waits for them, and re-layouts: 3.51 us -> 0 us
    pallas_call x1, Pallas kernels: 128 us -> 116 us  [field(): pl.pallas_call(field_kernel, out_shape=(jax.ShapeDtypeStruct((ROWS, N), F...]
    unnamed x7 -> x0, local copies, waits for them, and re-layouts: 3.51 us -> none
where the time goes in v2:
time: 121 us
  Pallas kernels  120 us (99%)
    pallas_call x1, Pallas kernels, field(): pl.pallas_call(field_kernel, out_shape=(jax.ShapeDtypeStruct((ROWS, N), F...  116 us
    pallas_call x1, Pallas kernels, written(): pl.pallas_call(write_kernel, out_shape=(jax.ShapeDtypeStruct((ROWS, N), F...  3.97 us

profile of v2, /device:TPU:0, one launch (start us, length us, event | category | flops | bytes accessed | tf_op | source)
XLA Modules:
  0.0 120.7 jit_solution(7024975898813214178)
XLA Ops:
  0.6 116.1 %field.1 = (f32[256,4096]{1,0:T(8,128)S(1)}, f32[256,4096]{1,0:T(8,128)S(1)}, f32[32,64]{1,0:T(8,128)S(1)}) custom-call(s32[2]{0:T(128)} %off_hbm.1, f32[256,4096]{1,0:T(8,128)} %bitcast.3, f32[4096,256]{1,0:T(8,128)} %amp_hbm.1, bf16[4,2,256,256]{3,2,1,0:T(8,128)(2,1)} %constant.4.clone.mats_hbm, f32[2,32,128]{2,1,0:T(8,128)} %constant.5.clone.tw_hbm), custom_call_target="tpu_custom_call" | custom-call | tf_op jit(solution)/shard_map/field/pallas_call | solution.py:516
  116.8 4.0 %write.1 = (f32[256,4096]{1,0:T(8,128)}, f32[256,4096]{1,0:T(8,128)}, f32[32,64]{1,0:T(8,128)}) custom-call(f32[256,4096]{1,0:T(8,128)S(1)} %get-tuple-element.9.tx, f32[256,4096]{1,0:T(8,128)S(1)} %get-tuple-element.10.ty, f32[32,64]{1,0:T(8,128)S(1)} %get-tuple-element.11.ratio), custom_call_target="tpu_custom_call" | custom-call | tf_op jit(solution)/shard_map/write/pallas_call | solution.py:581

commit v3 on v2

--- a/solution.py
+++ b/solution.py
@@ -164,12 +164,6 @@
     gx, me = lax.axis_index("gx"), lax.axis_index("gy")
     north = lax.rem(me + G - 1, G)
 
-    barrier = pltpu.get_barrier_semaphore()
-    for o in ORDER:
-        pl.semaphore_signal(barrier, inc=1, device_id={"gy": lax.rem(me + o, G)}, device_id_type=MESH)
-    for o in range(1, GX):
-        pl.semaphore_signal(barrier, inc=1, device_id={"gx": lax.rem(gx + o, GX)}, device_id_type=MESH)
-
     x_parts = [
         pltpu.make_async_copy(x_hbm.at[pl.ds(32 * i, 32)], p_v.at[pl.ds(32 * i, 32)], x_sem.at[i])
         for i in range(8)
@@ -177,13 +171,17 @@
     mats_cp = pltpu.make_async_copy(mats_hbm, mats, amp_sem.at[2])
     tw_cp = pltpu.make_async_copy(tw_hbm, tw, amp_sem.at[3])
     off_cp = pltpu.make_async_copy(off_hbm, off, amp_sem.at[4])
-    x_parts[0].start()
     tw_cp.start()
-    x_parts[1].start()
+    for cp in x_parts:
+        cp.start()
+
+    barrier = pltpu.get_barrier_semaphore()
+    for o in ORDER:
+        pl.semaphore_signal(barrier, inc=1, device_id={"gy": lax.rem(me + o, G)}, device_id_type=MESH)
+    for o in range(1, GX):
+        pl.semaphore_signal(barrier, inc=1, device_id={"gx": lax.rem(gx + o, GX)}, device_id_type=MESH)
     mats_cp.start()
     off_cp.start()
-    for cp in x_parts[2:]:
-        cp.start()
     amp_parts = [
         pltpu.make_async_copy(amp_hbm.at[:, pl.ds(L * h, L)], pr_v.at[0, pl.ds(N * h, N)], amp_sem.at[h]) for h in range(2)
     ]
@@ -202,65 +200,82 @@
             a_v[k, rows, L:] = a * s + b * c
         return carry
 
-    def first_copy(chunk, o):
+    def first_refs(part, d):
+        if part < 2:
+            return send1.at[d, 0, part], recv1.at[0, me, part]
+        return send1.at[d, part - 1], recv1.at[part - 1, me]
+
+    def first_copy(part, o):
         d = lax.rem(me + o, G)
+        src, dst = first_refs(part, d)
         return pltpu.make_async_remote_copy(
-            src_ref=send1.at[d, chunk], dst_ref=recv1.at[chunk, me],
-            send_sem=s1_sem.at[chunk, o], recv_sem=r1_sem.at[chunk, o],
+            src_ref=src, dst_ref=dst, send_sem=s1_sem.at[part, o], recv_sem=r1_sem.at[part, o],
             device_id={"gy": d}, device_id_type=MESH,
         )
 
-    def first_own(chunk):
-        return pltpu.make_async_copy(send1.at[me, chunk], recv1.at[chunk, me], r1_sem.at[chunk, 0])
-
-    def send_first(chunk):
+    def first_own(part):
+        src, dst = first_refs(part, me)
+        return pltpu.make_async_copy(src, dst, r1_sem.at[part, 0])
+
+    def send_first(part):
         for o in ORDER:
-            first_copy(chunk, o).start()
-        first_own(chunk).start()
-
-    def second_copy(half, chunk, o):
+            first_copy(part, o).start()
+        first_own(part).start()
+
+    def second_refs(part, chunk, d):
+        if part == 0:
+            return send2.at[d, 0, chunk], recv2.at[0, chunk, me]
+        pairs = pl.ds(PER // 2 * (part - 1), PER // 2)
+        return send2.at[d, 1, chunk, pairs], recv2.at[1, chunk, me, pairs]
+
+    def second_copy(part, chunk, o):
         d = lax.rem(me + o, G)
+        src, dst = second_refs(part, chunk, d)
         return pltpu.make_async_remote_copy(
-            src_ref=send2.at[d, half, chunk], dst_ref=recv2.at[half, chunk, me],
-            send_sem=s2_sem.at[half, chunk, o], recv_sem=r2_sem.at[half, chunk, o],
+            src_ref=src, dst_ref=dst,
+            send_sem=s2_sem.at[part, chunk, o], recv_sem=r2_sem.at[part, chunk, o],
             device_id={"gy": d}, device_id_type=MESH,
         )
 
-    def second_own(half, chunk):
-        return pltpu.make_async_copy(
-            send2.at[me, half, chunk], recv2.at[half, chunk, me], r2_sem.at[half, chunk, 0]
-        )
-
-    def send_second(half, chunk):
+    def second_own(part, chunk):
+        src, dst = second_refs(part, chunk, me)
+        return pltpu.make_async_copy(src, dst, r2_sem.at[part, chunk, 0])
+
+    def send_second(part, chunk):
         for o in ORDER:
-            second_copy(half, chunk, o).start()
-        second_own(half, chunk).start()
-
-    def x_lanes(j, carry, chunk):
+            second_copy(part, chunk, o).start()
+        second_own(part, chunk).start()
+
+    def x_lanes(j, carry, chunk, halves):
         slot = slot_of(chunk, j)
         which = jnp.where(slot == 0, 2, 1)
-        hi, lo = split(a_v[slot])
+        data = a_v[slot] if len(halves) == 2 else a_v[slot, L * halves[0] : L * (halves[0] + 1), :]
+        hi, lo = split(data)
         w_hi, w_lo = mats[which, 0], mats[which, 1]
         o = dot(w_hi, hi, True) + (dot(w_hi, lo, True) + dot(w_lo, hi, True))
-        for h in range(2):
+        for n, h in enumerate(halves):
             for c in range(2):
                 for d in range(G):
                     r = (c * G + d) * 8
-                    send1[d, chunk, h, j, c] = o[r : r + 8, L * h : L * (h + 1)]
+                    send1[d, chunk, h, j, c] = o[r : r + 8, L * n : L * (n + 1)]
         return carry
 
-    for i in range(8):
-        x_parts[i].wait()
-        if i == 0:
-            tw_cp.wait()
-        lax.fori_loop(4 * i, 4 * i + 4, x_tiles, 0)
-    mats_cp.wait()
-    off_cp.wait()
-    for chunk in range(CHUNKS):
-        lax.fori_loop(0, PER, functools.partial(x_lanes, chunk=chunk), 0)
-        if chunk == 0:
+    for h in range(2):
+        for i in range(4 * h, 4 * h + 4):
+            x_parts[i].wait()
+            if i == 0:
+                tw_cp.wait()
+            lax.fori_loop(4 * i, 4 * i + 4, x_tiles, 0)
+        if h == 0:
+            mats_cp.wait()
+            off_cp.wait()
+        lax.fori_loop(0, PER, functools.partial(x_lanes, chunk=0, halves=(h,)), 0)
+        if h == 0:
             pl.semaphore_wait(barrier, G - 1 + GX - 1)
-        send_first(chunk)
+        send_first(h)
+    for chunk in range(1, CHUNKS):
+        lax.fori_loop(0, PER, functools.partial(x_lanes, chunk=chunk, halves=(0, 1)), 0)
+        send_first(chunk + 1)
 
     for cp in amp_parts:
         cp.wait()
@@ -297,10 +312,12 @@
         0.0,
     ).astype(BF16)
 
+    lower = lax.broadcasted_iota(jnp.int32, (8, L), 1) < L // 2
     for chunk in range(CHUNKS):
-        for o in ORDER:
-            first_copy(chunk, o).wait_recv()
-        first_own(chunk).wait()
+        for part in (0, 1) if chunk == 0 else (chunk + 1,):
+            for o in ORDER:
+                first_copy(part, o).wait_recv()
+            first_own(part).wait()
 
         def y_tiles(j, carry, chunk=chunk):
             rows = pl.ds(pl.multiple_of(8 * j, 8), 8)
@@ -371,21 +388,47 @@
                     send2[t // 2, t % 2, CHUNKS - 1, 0, 1, 0:1, :] = out[t][1][0:1, :]
 
         send_second(0, chunk)
-    for chunk in range(CHUNKS):
-        send_second(1, chunk)
-
-    def x_back(j, carry, half, chunk):
+
+        def pack(d, carry, chunk=chunk):
+            for c in range(2):
+                v = [send2[d, 1, chunk, j, c] for j in range(PER)]
+                w = [pltpu.roll(one, L // 2, 1) for one in v]
+                for n in range(PER // 2):
+                    send2[d, 1, chunk, n, c] = jnp.where(lower, v[2 * n], w[2 * n + 1])
+                    send2[d, 1, chunk, PER // 2 + n, c] = jnp.where(lower, w[2 * n], v[2 * n + 1])
+            return carry
+
+        lax.fori_loop(0, G, pack, 0)
+    for part in range(1, 3):
+        for chunk in range(CHUNKS):
+            send_second(part, chunk)
+
+    def put_back(slot, rows, o):
+        a, b = o[:, :L], o[:, L:]
+        c, s = tw[0, pl.ds(slot, 1), :], tw[1, pl.ds(slot, 1), :]
+        a_v[slot, rows, :L] = a * c + b * s
+        a_v[slot, rows, L:] = b * c - a * s
+
+    def x_back(j, carry, chunk):
         slot = slot_of(chunk, j)
         data = jnp.concatenate(
-            [recv2[half, chunk, d, j, c] for c in range(2) for d in range(G)], axis=0
+            [recv2[0, chunk, d, j, c] for c in range(2) for d in range(G)], axis=0
         )
-        which = jnp.where(slot == 0, 3, 1)
-        o = dot3(data.T, mats, which)
-        a, b = o[:, :L], o[:, L:]
-        c, s = tw[0, pl.ds(slot, 1), :], tw[1, pl.ds(slot, 1), :]
-        a_v[slot, L * half : L * (half + 1), :L] = a * c + b * s
-        a_v[slot, L * half : L * (half + 1), L:] = b * c - a * s
+        put_back(slot, slice(0, L), dot3(data.T, mats, jnp.where(slot == 0, 3, 1)))
         return carry
+
+    def x_back_pairs(part, chunk):
+        half = L // 2
+        rows = slice(L + half * (part - 1), L + half * part)
+        for n in range(PER // 2):
+            slot = slot_of(chunk, 2 * n)
+            at = PER // 2 * (part - 1) + n
+            data = jnp.concatenate(
+                [recv2[1, chunk, d, at, c] for c in range(2) for d in range(G)], axis=0
+            ).T
+            o = dot3(data, mats, 1)
+            put_back(slot, rows, dot3(data[:half], mats, 3) if slot == 0 else o[:half])
+            put_back(slot + 1, rows, o[half:])
 
     def x_last(i, carry):
         rows = pl.ds(pl.multiple_of(8 * i, 8), 8)
@@ -401,15 +444,15 @@
             pr_v[1, here, :] = 1.0 / p
         return carry
 
-    def y_sums(t, carry, half):
+    def y_sums(t, carry, first, count):
         for v in range(2):
-            up, low = jnp.zeros((16, L), F32), jnp.zeros((16, L), F32)
+            up, low = jnp.zeros((count, L), F32), jnp.zeros((count, L), F32)
             for a in range(8):
-                u = pr_v[v, pl.ds(ROWS * t + L * half + a, 16, stride=8), :]
+                u = pr_v[v, pl.ds(ROWS * t + 8 * first + a, count, stride=8), :]
                 up += jnp.where(a >= shift_y, u, 0.0)
                 low += jnp.where(a < shift_y, u, 0.0)
-            up_s[v, t, 16 * half : 16 * half + 16, :] = up
-            low_s[v, t, 16 * half : 16 * half + 16, :] = low
+            up_s[v, t, first : first + count, :] = up
+            low_s[v, t, first : first + count, :] = low
         return carry
 
     lane_end = lax.broadcasted_iota(jnp.int32, (8, L), 1) == L - 1
@@ -431,27 +474,34 @@
         src_ref=halo_s, dst_ref=halo_r, send_sem=m_sem.at[2], recv_sem=m_sem.at[3],
         device_id={"gy": north}, device_id_type=MESH,
     )
-    g = gsel[...]
-
     def along_x(rows):
-        outs = []
+        parts = []
         for b in range(4):
             nxt = 1024 * (b + 1) % N
             lanes = [sum_s[rows, 1024 * b : 1024 * (b + 1)], sum_s[rows, nxt : nxt + L]]
-            hi, lo = split(jnp.concatenate(lanes, axis=1))
-            outs.append(dot(hi, g) + dot(lo, g))
-        return outs
+            parts.append(jnp.concatenate(lanes, axis=1))
+        data = jnp.concatenate(parts, axis=0)
+        hi, lo = split(data)
+        out = dot(jnp.concatenate([hi, lo], axis=0), gsel[...])
+        out = out[: data.shape[0]] + out[data.shape[0] :]
+        n = data.shape[0] // 4
+        return [out[n * b : n * (b + 1)] for b in range(4)]
 
     last_row = lax.broadcasted_iota(jnp.int32, (T, L), 0) == T - 1
-    for half in range(2):
+    for part, (first, count) in enumerate(((0, 16), (16, 8), (24, 8))):
         for chunk in range(CHUNKS):
             for o in ORDER:
-                second_copy(half, chunk, o).wait_recv()
-            second_own(half, chunk).wait()
-            lax.fori_loop(0, PER, functools.partial(x_back, half=half, chunk=chunk), 0)
-        lax.fori_loop(16 * half, 16 * half + 16, x_last, 0)
-        lax.fori_loop(0, T, functools.partial(y_sums, half=half), 0)
-        if half == 0:
+                second_copy(part, chunk, o).wait_recv()
+            second_own(part, chunk).wait()
+            if part == 0:
+                lax.fori_loop(0, PER, functools.partial(x_back, chunk=chunk), 0)
+            else:
+                x_back_pairs(part, chunk)
+        lax.fori_loop(first, first + count, x_last, 0)
+        lax.fori_loop(0, T, functools.partial(y_sums, first=first, count=count), 0)
+        if part == 1:
+            lax.fori_loop(15, 23, trans, 0)
+        if part == 0:
             for t in range(T):
                 halo_s[t : t + 1, :] = p_v[0:1, L * t : L * (t + 1)]
                 for v in range(2):
@@ -468,45 +518,45 @@
             sum_s[T * v : T * v + T, L * t : L * (t + 1)] = up_s[v, t] + moved
     halo_cp.wait()
     for b, out in enumerate(along_x(slice(0, 2 * T))):
+        both = []
         for v in range(2):
             lead = jnp.broadcast_to(halo_r[T + 2 * b + v : T + 2 * b + v + 1, :], (T, L))
-            bs_main[b, v] = out[T * v : T * v + T, :] + jnp.where(last_row, lead, 0.0)
+            both.append(out[T * v : T * v + T, :] + jnp.where(last_row, lead, 0.0))
+        for h in range(2):
+            mine = slice(L // 2 * h, L // 2 * (h + 1))
+            bs_main[2 * b + h] = jnp.concatenate([v[:, mine] for v in both], axis=1)
 
     def main_copy(o):
         peer = lax.rem(gx + o, GX)
         return pltpu.make_async_remote_copy(
-            src_ref=bs_main.at[peer // 2], dst_ref=in_main.at[gx],
+            src_ref=bs_main.at[peer], dst_ref=in_main.at[gx],
             send_sem=m_sem.at[8 + o], recv_sem=m_sem.at[16 + o],
             device_id={"gx": peer}, device_id_type=MESH,
         )
 
-    own_main = pltpu.make_async_copy(bs_main.at[gx // 2], in_main.at[gx], m_sem.at[16])
+    own_main = pltpu.make_async_copy(bs_main.at[gx], in_main.at[gx], m_sem.at[16])
     own_main.start()
     for o in range(1, GX):
         main_copy(o).start()
     for t in range(T):
         p_v[ROWS : ROWS + 1, L * t : L * (t + 1)] = halo_r[t : t + 1, :]
 
-    lax.fori_loop(15, 32, trans, 0)
-    for chunk in range(CHUNKS):
+    lax.fori_loop(23, 32, trans, 0)
+    for part in range(CHUNKS + 1):
         for o in ORDER:
-            first_copy(chunk, o).wait_send()
-    for half in range(2):
+            first_copy(part, o).wait_send()
+    for part in range(3):
         for chunk in range(CHUNKS):
             for o in ORDER:
-                second_copy(half, chunk, o).wait_send()
+                second_copy(part, chunk, o).wait_send()
 
     own_main.wait()
     for o in range(1, GX):
         main_copy(o).wait()
-    sums = []
-    for v in range(2):
-        main = in_main[0, v]
-        for g_ in range(1, GX):
-            main += in_main[g_, v]
-        sums.append(main)
-    ratio = sums[0] / sums[1]
-    ratio_out[...] = jnp.where(lax.rem(gx, 2) == 0, ratio[:, : L // 2], ratio[:, L // 2 :])
+    sums = in_main[0]
+    for g in range(1, GX):
+        sums += in_main[g]
+    ratio_out[...] = sums[:, : L // 2] / sums[:, L // 2 :]
 
 
 def field(off, x, amp, mats, tw):
@@ -535,24 +585,24 @@
             pltpu.VMEM((T, 8 * PER, 2 * L), F32),
             pltpu.VMEM((T, 8, 2 * L), F32),
             pltpu.VMEM((T, 8 * SLOTS, L), F32),
-            pltpu.VMEM((2 * L, L), F32),
+            pltpu.VMEM((2 * L + 16, L), F32),
             pltpu.VMEM((T, L), F32),
             pltpu.VMEM((T, L), F32),
-            pltpu.VMEM((2, T * ROWS, L), F32),
+            pltpu.VMEM((2, T * ROWS + 32, L), F32),
             pltpu.VMEM((2, T, T, L), F32),
             pltpu.VMEM((2, T, T, L), F32),
             pltpu.VMEM((2 * T, N), F32),
             pltpu.VMEM((T + 8, L), F32),
             pltpu.VMEM((T + 8, L), F32),
-            pltpu.VMEM((4, 2, T, L), F32),
-            pltpu.VMEM((GX, 2, T, L), F32),
+            pltpu.VMEM((GX, T, L), F32),
+            pltpu.VMEM((GX, T, L), F32),
             pltpu.VMEM((1024 + L, L), BF16),
             pltpu.SemaphoreType.DMA((8,)),
             pltpu.SemaphoreType.DMA((5,)),
-            pltpu.SemaphoreType.DMA((CHUNKS, G)),
-            pltpu.SemaphoreType.DMA((CHUNKS, G)),
-            pltpu.SemaphoreType.DMA((2, CHUNKS, G)),
-            pltpu.SemaphoreType.DMA((2, CHUNKS, G)),
+            pltpu.SemaphoreType.DMA((CHUNKS + 1, G)),
+            pltpu.SemaphoreType.DMA((CHUNKS + 1, G)),
+            pltpu.SemaphoreType.DMA((3, CHUNKS, G)),
+            pltpu.SemaphoreType.DMA((3, CHUNKS, G)),
             pltpu.SemaphoreType.DMA((24,)),
         ],
         compiler_params=pltpu.CompilerParams(

time: 121 us -> 119 us (0.983)
  Pallas kernels: 120 us -> 118 us
    pallas_call x1, Pallas kernels: 116 us -> 114 us  [field(): pl.pallas_call(field_kernel, out_shape=(jax.ShapeDtypeStruct((ROWS, N), F...]
where the time goes in v3:
time: 119 us
  Pallas kernels  118 us (99%)
    pallas_call x1, Pallas kernels, field(): pl.pallas_call(field_kernel, out_shape=(jax.ShapeDtypeStruct((ROWS, N), F...  114 us
    pallas_call x1, Pallas kernels, written(): pl.pallas_call(write_kernel, out_shape=(jax.ShapeDtypeStruct((ROWS, N), F...  3.97 us

profile of v3, /device:TPU:0, one launch (start us, length us, event | category | flops | bytes accessed | tf_op | source)
XLA Modules:
  0.0 118.5 jit_solution(5243085602285045730)
XLA Ops:
  0.6 113.9 %field.1 = (f32[256,4096]{1,0:T(8,128)S(1)}, f32[256,4096]{1,0:T(8,128)S(1)}, f32[32,64]{1,0:T(8,128)S(1)}) custom-call(s32[2]{0:T(128)} %off_hbm.1, f32[256,4096]{1,0:T(8,128)} %bitcast.3, f32[4096,256]{1,0:T(8,128)} %amp_hbm.1, bf16[4,2,256,256]{3,2,1,0:T(8,128)(2,1)} %constant.4.clone.mats_hbm, f32[2,32,128]{2,1,0:T(8,128)} %constant.5.clone.tw_hbm), custom_call_target="tpu_custom_call" | custom-call | tf_op jit(solution)/shard_map/field/pallas_call | solution.py:566
  114.6 4.0 %write.1 = (f32[256,4096]{1,0:T(8,128)}, f32[256,4096]{1,0:T(8,128)}, f32[32,64]{1,0:T(8,128)}) custom-call(f32[256,4096]{1,0:T(8,128)S(1)} %get-tuple-element.9.tx, f32[256,4096]{1,0:T(8,128)S(1)} %get-tuple-element.10.ty, f32[32,64]{1,0:T(8,128)S(1)} %get-tuple-element.11.ratio), custom_call_target="tpu_custom_call" | custom-call | tf_op jit(solution)/shard_map/write/pallas_call | solution.py:631

commit v4 on v3

--- a/solution.py
+++ b/solution.py
@@ -265,11 +265,11 @@
             x_parts[i].wait()
             if i == 0:
                 tw_cp.wait()
-            lax.fori_loop(4 * i, 4 * i + 4, x_tiles, 0)
+            lax.fori_loop(4 * i, 4 * i + 4, x_tiles, 0, unroll=2)
         if h == 0:
             mats_cp.wait()
             off_cp.wait()
-        lax.fori_loop(0, PER, functools.partial(x_lanes, chunk=0, halves=(h,)), 0)
+        lax.fori_loop(0, PER, functools.partial(x_lanes, chunk=0, halves=(h,)), 0, unroll=True)
         if h == 0:
             pl.semaphore_wait(barrier, G - 1 + GX - 1)
         send_first(h)
@@ -402,6 +402,15 @@
     for part in range(1, 3):
         for chunk in range(CHUNKS):
             send_second(part, chunk)
+    for part in range(CHUNKS + 1):
+        for o in ORDER:
+            first_copy(part, o).wait_send()
+
+    def sent(part):
+        for chunk in range(CHUNKS):
+            for o in ORDER:
+                second_copy(part, chunk, o).wait_send()
+
 
     def put_back(slot, rows, o):
         a, b = o[:, :L], o[:, L:]
@@ -497,10 +506,11 @@
                 lax.fori_loop(0, PER, functools.partial(x_back, chunk=chunk), 0)
             else:
                 x_back_pairs(part, chunk)
-        lax.fori_loop(first, first + count, x_last, 0)
-        lax.fori_loop(0, T, functools.partial(y_sums, first=first, count=count), 0)
+        lax.fori_loop(first, first + count, x_last, 0, unroll=2)
+        lax.fori_loop(0, T, functools.partial(y_sums, first=first, count=count), 0, unroll=4)
         if part == 1:
             lax.fori_loop(15, 23, trans, 0)
+            sent(1)
         if part == 0:
             for t in range(T):
                 halo_s[t : t + 1, :] = p_v[0:1, L * t : L * (t + 1)]
@@ -511,6 +521,7 @@
                 halo_s[T + 2 * b : T + 2 * b + 2, :] = out[0:2]
             halo_cp.start()
             lax.fori_loop(0, 15, trans, 0)
+            sent(0)
 
     for t in range(T):
         for v in range(2):
@@ -542,17 +553,11 @@
         p_v[ROWS : ROWS + 1, L * t : L * (t + 1)] = halo_r[t : t + 1, :]
 
     lax.fori_loop(23, 32, trans, 0)
-    for part in range(CHUNKS + 1):
-        for o in ORDER:
-            first_copy(part, o).wait_send()
-    for part in range(3):
-        for chunk in range(CHUNKS):
-            for o in ORDER:
-                second_copy(part, chunk, o).wait_send()
 
     own_main.wait()
     for o in range(1, GX):
         main_copy(o).wait()
+    sent(2)
     sums = in_main[0]
     for g in range(1, GX):
         sums += in_main[g]

time: 119 us -> 119 us (level)
  no operation moved by 1% of the time
where the time goes in v4:
time: 119 us; the launch traced here: 118 us
  Pallas kernels  117 us (98%)
    pallas_call x1, Pallas kernels, field(): pl.pallas_call(field_kernel, out_shape=(jax.ShapeDtypeStruct((ROWS, N), F...  113 us
    pallas_call x1, Pallas kernels, written(): pl.pallas_call(write_kernel, out_shape=(jax.ShapeDtypeStruct((ROWS, N), F...  3.97 us

profile of v4, /device:TPU:0, one launch (start us, length us, event | category | flops | bytes accessed | tf_op | source)
XLA Modules:
  0.0 118.0 jit_solution(1578217650182573687)
XLA Ops:
  0.6 113.3 %field.1 = (f32[256,4096]{1,0:T(8,128)S(1)}, f32[256,4096]{1,0:T(8,128)S(1)}, f32[32,64]{1,0:T(8,128)S(1)}) custom-call(s32[2]{0:T(128)} %off_hbm.1, f32[256,4096]{1,0:T(8,128)} %bitcast.3, f32[4096,256]{1,0:T(8,128)} %amp_hbm.1, bf16[4,2,256,256]{3,2,1,0:T(8,128)(2,1)} %constant.4.clone.mats_hbm, f32[2,32,128]{2,1,0:T(8,128)} %constant.5.clone.tw_hbm), custom_call_target="tpu_custom_call" | custom-call | tf_op jit(solution)/shard_map/field/pallas_call | solution.py:571
  113.9 4.0 %write.1 = (f32[256,4096]{1,0:T(8,128)}, f32[256,4096]{1,0:T(8,128)}, f32[32,64]{1,0:T(8,128)}) custom-call(f32[256,4096]{1,0:T(8,128)S(1)} %get-tuple-element.9.tx, f32[256,4096]{1,0:T(8,128)S(1)} %get-tuple-element.10.ty, f32[32,64]{1,0:T(8,128)S(1)} %get-tuple-element.11.ratio), custom_call_target="tpu_custom_call" | custom-call | tf_op jit(solution)/shard_map/write/pallas_call | solution.py:636

commit v5 on v4

--- a/solution.py
+++ b/solution.py
@@ -156,7 +156,7 @@
 
 def field_kernel(
     off_hbm, x_hbm, amp_hbm, mats_hbm, tw_hbm,
-    tx_out, ty_out, ratio_out,
+    tx_out, ty_out, sums_out,
     off, tw, mats, p_v, a_v, send1, recv1, send2, recv2, z_v, z2_v, amp_t, tmp_t, nyq, nyq_in, pr_v,
     up_s, low_s, sum_s, halo_s, halo_r, bs_main, in_main, gsel,
     x_sem, amp_sem, s1_sem, r1_sem, s2_sem, r2_sem, m_sem,
@@ -507,7 +507,7 @@
             else:
                 x_back_pairs(part, chunk)
         lax.fori_loop(first, first + count, x_last, 0, unroll=2)
-        lax.fori_loop(0, T, functools.partial(y_sums, first=first, count=count), 0, unroll=4)
+        lax.fori_loop(0, T, functools.partial(y_sums, first=first, count=count), 0, unroll=8)
         if part == 1:
             lax.fori_loop(15, 23, trans, 0)
             sent(1)
@@ -561,7 +561,7 @@
     sums = in_main[0]
     for g in range(1, GX):
         sums += in_main[g]
-    ratio_out[...] = sums[:, : L // 2] / sums[:, L // 2 :]
+    sums_out[...] = sums
 
 
 def field(off, x, amp, mats, tw):
@@ -573,7 +573,7 @@
         out_shape=(
             jax.ShapeDtypeStruct((ROWS, N), F32),
             jax.ShapeDtypeStruct((ROWS, N), F32),
-            jax.ShapeDtypeStruct((T, L // 2), F32),
+            jax.ShapeDtypeStruct((T, L), F32),
         ),
         in_specs=[hbm] * 5,
         out_specs=(vmem, vmem, vmem),
@@ -617,7 +617,7 @@
     )(*(pltpu.with_memory_space_constraint(v, pltpu.HBM) for v in (off, x, amp, mats, tw)))
 
 
-def write_kernel(tx, ty, ratio, tx_out, ty_out, up_out, sem):
+def write_kernel(tx, ty, sums, tx_out, ty_out, up_out, sem):
     copies = []
     for n, (src, dst) in enumerate(((tx, tx_out), (ty, ty_out))):
         for i in range(4):
@@ -625,7 +625,7 @@
             copies.append(pltpu.make_async_copy(src.at[rows], dst.at[rows], sem.at[4 * n + i]))
     for cp in copies:
         cp.start()
-    up_out[...] = jnp.sqrt(ratio[...])
+    up_out[...] = jnp.sqrt(sums[:, : L // 2] / sums[:, L // 2 :])
     for cp in copies:
         cp.wait()
 

time: 119 us -> 118 us (level)
  no operation moved by 1% of the time
where the time goes in v5:
time: 118 us
  Pallas kernels  117 us (99%)
    pallas_call x1, Pallas kernels, field(): pl.pallas_call(field_kernel, out_shape=(jax.ShapeDtypeStruct((ROWS, N), F...  113 us
    pallas_call x1, Pallas kernels, written(): pl.pallas_call(write_kernel, out_shape=(jax.ShapeDtypeStruct((ROWS, N), F...  3.97 us

profile of v5, /device:TPU:0, one launch (start us, length us, event | category | flops | bytes accessed | tf_op | source)
XLA Modules:
  0.0 117.9 jit_solution(17715622893160527902)
XLA Ops:
  0.6 113.2 %field.1 = (f32[256,4096]{1,0:T(8,128)S(1)}, f32[256,4096]{1,0:T(8,128)S(1)}, f32[32,128]{1,0:T(8,128)S(1)}) custom-call(s32[2]{0:T(128)} %off_hbm.1, f32[256,4096]{1,0:T(8,128)} %bitcast.3, f32[4096,256]{1,0:T(8,128)} %amp_hbm.1, bf16[4,2,256,256]{3,2,1,0:T(8,128)(2,1)} %constant.4.clone.mats_hbm, f32[2,32,128]{2,1,0:T(8,128)} %constant.5.clone.tw_hbm), custom_call_target="tpu_custom_call" | custom-call | tf_op jit(solution)/shard_map/field/pallas_call | solution.py:571
  113.8 4.0 %write.1 = (f32[256,4096]{1,0:T(8,128)}, f32[256,4096]{1,0:T(8,128)}, f32[32,64]{1,0:T(8,128)}) custom-call(f32[256,4096]{1,0:T(8,128)S(1)} %get-tuple-element.9.tx, f32[256,4096]{1,0:T(8,128)S(1)} %get-tuple-element.10.ty, f32[32,128]{1,0:T(8,128)S(1)} %get-tuple-element.11.sums), custom_call_target="tpu_custom_call" | custom-call | tf_op jit(solution)/shard_map/write/pallas_call | solution.py:636
